TPU v7x, 32 devices: a whole 2x2x4 slice. The times are simulated.
32 devices in a mesh: dp: 8 (over y, x, core), mp: 4 (over z).
Axes of the slice: x: 2, y: 2, z: 4, core: 2. Of those that a mesh axis runs over, the one named last changes fastest.
Arguments:
- stream: float32 [16384, 768], P('dp', 'mp'), may hold values from -6 to 6
- seq_lens: int32 [32], P('dp'), may hold values from 0 to 2048, as said below
- w_qkv: bfloat16 [2, 768, 3, 768], P(None, None, None, 'mp'), may hold values from -0.3125 to 0.3125
- b_qv: float32 [2, 2, 768], P(None, None, 'mp'), may hold values from -3 to 3
- w_out: bfloat16 [2, 768, 768], P(None, 'mp'), may hold values from -0.625 to 0.625
- b_out: float32 [2, 768], P(None, 'mp'), may hold values from -2 to 2
- w_up: bfloat16 [2, 768, 3072], P(None, None, 'mp'), may hold values from -0.21875 to 0.21875
- b_up: float32 [2, 3072], P(None, 'mp'), may hold values from -3 to 3
- w_down: bfloat16 [2, 3072, 768], P(None, 'mp'), may hold values from -0.15625 to 0.15625
- b_down: float32 [2, 768], P(None, 'mp'), may hold values from -2 to 2
- cotangent: float32 [16384, 768], P('dp', 'mp'), may hold values from -6 to 6
Outputs:
- out_first: float32 [16384, 768], P('dp', 'mp')
- out_second: float32 [16384, 768], P('dp', 'mp')
- grad_stream: float32 [16384, 768], P('dp', 'mp')
- grad_w_qkv: float32 [2, 768, 3, 768], P(None, None, None, 'mp')
- grad_b_qv: float32 [2, 2, 768], P(None, None, 'mp')
- grad_w_out: float32 [2, 768, 768], P(None, 'mp')
- grad_b_out: float32 [2, 768], P(None, 'mp')
- grad_w_up: float32 [2, 768, 3072], P(None, None, 'mp')
- grad_b_up: float32 [2, 3072], P(None, 'mp')
- grad_w_down: float32 [2, 3072, 768], P(None, 'mp')
- grad_b_down: float32 [2, 768], P(None, 'mp')
Inputs may be any that keep to these rules, and one draw needn't show every extreme that they name: `seq_lens`: each index of dp holds 2048 tokens in its 4 entries: either one sequence of 2048 tokens followed by zeros, or 4 sequences of 512 tokens; exactly half of the indices hold the single sequence, which ones is drawn from the seed.
All inputs are finite; a program needn't handle non-finite values.
Results may differ from a plain program's by a relative error of at most 0.029.
Values may be sent and summed in bfloat16 or wider, within the bound.
No kernel may reach another device: no remote copies, remote signals or barrier semaphores. Data moves between devices by JAX's collectives and lax.ppermute only.
A program may use at most 256 MiB of HBM per device.

v0:
```python
import jax
import jax.numpy as jnp
from jax import lax
from jax.sharding import PartitionSpec as P

D = 768
HEADS = 12


EPS = 1e-06
CONTRACT_ROWS = (((0,), (0,)), ((), ()))
CONTRACT_COLS = (((1,), (1,)), ((), ()))


def norm_stats(stream_now, full_width):
    totals, squares = lax.psum(
        (jnp.sum(stream_now, axis=1), jnp.sum(stream_now * stream_now, axis=1)), "mp"
    )
    return (totals, lax.rsqrt((squares + totals * totals) / full_width + EPS))


def norm_grad(stream_now, totals, factor, d_normed, full_width):
    inner_sum = lax.psum(jnp.sum(d_normed * stream_now, axis=1), "mp")
    factor_term = factor * factor * factor * inner_sum / full_width
    return factor[:, None] * d_normed - factor_term[:, None] * (stream_now + totals[:, None])


def project_in(normed, weight):
    gathered = lax.all_gather(normed, "mp", axis=1, tiled=True)
    return (gathered, jnp.dot(gathered, weight, preferred_element_type=jnp.float32))


def weight_grad(gathered, grad_rows):
    return lax.dot_general(gathered, grad_rows, CONTRACT_ROWS, preferred_element_type=jnp.float32)


def branch_sum(local_rows, weight):
    return lax.psum_scatter(
        jnp.dot(local_rows, weight, preferred_element_type=jnp.float32).astype(jnp.bfloat16),
        "mp",
        scatter_dimension=1,
        tiled=True,
    ).astype(jnp.float32)


def branch_spread(grad_rows):
    return lax.all_gather(grad_rows, "mp", axis=1, tiled=True)


def input_sum(grad_rows, weight):
    return lax.psum_scatter(
        lax.dot_general(
            grad_rows, weight, CONTRACT_COLS, preferred_element_type=jnp.float32
        ).astype(jnp.bfloat16),
        "mp",
        scatter_dimension=1,
        tiled=True,
    ).astype(jnp.float32)


def masked_scores(
    query_rows, key_rows, row_positions, key_positions, row_segment, key_segment, score_scale
):
    scores = (
        jnp.einsum("qhe,khe->hqk", query_rows, key_rows, preferred_element_type=jnp.float32)
        * score_scale
    )
    allowed = (row_segment[:, None] == key_segment[None, :]) & (
        row_positions[:, None] >= key_positions[None, :]
    )
    return jnp.where(allowed[None], scores, -1e30)


def attend_forward(queries, keys_all, values_all, segment, score_scale):
    length = queries.shape[0]
    block_rows = min(512, length)
    positions = jnp.arange(length, dtype=jnp.int32)
    results = []
    log_sums = []
    for block_index in range(length // block_rows):
        row_first = block_index * block_rows
        row_end = row_first + block_rows
        scores = masked_scores(
            queries[row_first:row_end],
            keys_all[:row_end],
            positions[row_first:row_end],
            positions[:row_end],
            segment[row_first:row_end],
            segment[:row_end],
            score_scale,
        )
        highest = jnp.max(scores, axis=2, keepdims=True)
        exponent = jnp.exp(scores - highest)
        totals = jnp.sum(exponent, axis=2, keepdims=True)
        chances = (exponent / totals).astype(jnp.bfloat16)
        results.append(
            jnp.einsum(
                "hqk,khe->qhe", chances, values_all[:row_end], preferred_element_type=jnp.float32
            )
        )
        log_sums.append((highest + jnp.log(totals))[:, :, 0])
    return (jnp.concatenate(results, axis=0), jnp.concatenate(log_sums, axis=1))


def attend_backward(queries, keys_all, values_all, segment, log_sums, d_heads, score_scale):
    length = queries.shape[0]
    block_rows = min(512, length)
    positions = jnp.arange(length, dtype=jnp.int32)
    query_grads = []
    key_grad = jnp.zeros(keys_all.shape, jnp.float32)
    value_grad = jnp.zeros(values_all.shape, jnp.float32)
    for block_index in range(length // block_rows):
        row_first = block_index * block_rows
        row_end = row_first + block_rows
        scores = masked_scores(
            queries[row_first:row_end],
            keys_all[:row_end],
            positions[row_first:row_end],
            positions[:row_end],
            segment[row_first:row_end],
            segment[:row_end],
            score_scale,
        )
        chances = jnp.exp(scores - log_sums[:, row_first:row_end, None])
        d_chances = jnp.einsum(
            "qhe,khe->hqk",
            d_heads[row_first:row_end],
            values_all[:row_end],
            preferred_element_type=jnp.float32,
        )
        inner_sum = jnp.sum(chances * d_chances, axis=2, keepdims=True)
        d_scores = (chances * (d_chances - inner_sum)).astype(jnp.bfloat16)
        query_grads.append(
            jnp.einsum(
                "hqk,khe->qhe", d_scores, keys_all[:row_end], preferred_element_type=jnp.float32
            )
            * score_scale
        )
        key_grad = key_grad.at[:row_end].add(
            jnp.einsum(
                "hqk,qhe->khe",
                d_scores,
                queries[row_first:row_end],
                preferred_element_type=jnp.float32,
            )
            * score_scale
        )
        value_grad = value_grad.at[:row_end].add(
            jnp.einsum(
                "hqk,qhe->khe",
                chances.astype(jnp.bfloat16),
                d_heads[row_first:row_end],
                preferred_element_type=jnp.float32,
            )
        )
    return (jnp.concatenate(query_grads, axis=0), key_grad, value_grad)


def gelu_tanh(argument):
    return jax.nn.gelu(argument, approximate=True)


def per_device(stream, seq_lens, w_qkv, b_qv, w_out, b_out, w_up, b_up, w_down, b_down, cotangent):
    length, local_width = stream.shape
    full_width = local_width * lax.axis_size("mp")
    head_size = D // HEADS
    heads_here = local_width // head_size
    score_scale = float(head_size) ** (-0.5)
    head_shape = (length, heads_here, head_size)
    columns = lax.axis_index("mp") * local_width + jnp.arange(local_width, dtype=jnp.int32)
    column_keep = (columns < full_width - 1).astype(jnp.float32)
    keep_narrow = column_keep.astype(jnp.bfloat16)
    bounds = jnp.cumsum(seq_lens, dtype=jnp.int32)
    positions = jnp.arange(length, dtype=jnp.int32)
    segment = jnp.sum((positions[:, None] >= bounds[None, :-1]).astype(jnp.int32), axis=1)
    layer_count = w_qkv.shape[0]
    stream_now = stream * column_keep
    stored = []
    layer_outs = []
    for layer_index in range(layer_count):
        residual = stream_now
        total_first, factor_first = norm_stats(residual, full_width)
        normed_first = (residual * factor_first[:, None]).astype(jnp.bfloat16)
        qkv_weight = w_qkv[layer_index].reshape(full_width, 3 * local_width)
        gathered_first, projected = project_in(normed_first, qkv_weight)
        projected = projected.reshape(length, 3, local_width)
        queries = (projected[:, 0] + b_qv[layer_index, 0]).astype(jnp.bfloat16).reshape(head_shape)
        keys_now = projected[:, 1].astype(jnp.bfloat16).reshape(head_shape)
        values_now = (
            (projected[:, 2] + b_qv[layer_index, 1]).astype(jnp.bfloat16).reshape(head_shape)
        )
        attended, log_sums = attend_forward(queries, keys_now, values_now, segment, score_scale)
        mixed_heads = attended.reshape(length, local_width).astype(jnp.bfloat16)
        branch = branch_sum(mixed_heads, w_out[layer_index])
        middle = residual + (branch + b_out[layer_index]) * column_keep
        total_second, factor_second = norm_stats(middle, full_width)
        normed_second = (middle * factor_second[:, None]).astype(jnp.bfloat16)
        gathered_second, hidden = project_in(normed_second, w_up[layer_index])
        hidden = hidden + b_up[layer_index]
        active = gelu_tanh(hidden).astype(jnp.bfloat16)
        branch_two = branch_sum(active, w_down[layer_index])
        stream_now = middle + (branch_two + b_down[layer_index]) * column_keep
        layer_outs.append(stream_now)
        stored.append(
            (
                residual,
                total_first,
                factor_first,
                normed_first,
                gathered_first,
                qkv_weight,
                queries,
                keys_now,
                values_now,
                log_sums,
                mixed_heads,
                middle,
                total_second,
                factor_second,
                normed_second,
                gathered_second,
                hidden,
                active,
            )
        )
    grad_now = cotangent
    collected = []
    for layer_index in reversed(range(layer_count)):
        (
            residual,
            total_first,
            factor_first,
            normed_first,
            gathered_first,
            qkv_weight,
            queries,
            keys_now,
            values_now,
            log_sums,
            mixed_heads,
            middle,
            total_second,
            factor_second,
            normed_second,
            gathered_second,
            hidden,
            active,
        ) = stored[layer_index]
        d_branch = grad_now.astype(jnp.bfloat16) * keep_narrow
        grad_bd = jnp.sum(d_branch, axis=0, dtype=jnp.float32)
        d_spread = branch_spread(d_branch)
        grad_wd = lax.dot_general(
            active, d_spread, CONTRACT_ROWS, preferred_element_type=jnp.float32
        )
        d_active = lax.dot_general(
            d_spread, w_down[layer_index], CONTRACT_COLS, preferred_element_type=jnp.float32
        )
        d_hidden = jax.vjp(gelu_tanh, hidden)[1](d_active)[0].astype(jnp.bfloat16)
        grad_bu = jnp.sum(d_hidden, axis=0, dtype=jnp.float32)
        grad_wu = weight_grad(gathered_second, d_hidden)
        d_normed = input_sum(d_hidden, w_up[layer_index])
        grad_mid = grad_now + norm_grad(middle, total_second, factor_second, d_normed, full_width)
        d_branch = grad_mid.astype(jnp.bfloat16) * keep_narrow
        grad_bo = jnp.sum(d_branch, axis=0, dtype=jnp.float32)
        d_spread = branch_spread(d_branch)
        grad_wo = lax.dot_general(
            mixed_heads, d_spread, CONTRACT_ROWS, preferred_element_type=jnp.float32
        )
        d_heads = lax.dot_general(
            d_spread, w_out[layer_index], CONTRACT_COLS, preferred_element_type=jnp.float32
        )
        d_heads = d_heads.astype(jnp.bfloat16).reshape(head_shape)
        d_query, d_key, d_value = attend_backward(
            queries, keys_now, values_now, segment, log_sums, d_heads, score_scale
        )
        d_qkv = jnp.stack(
            [
                d_query.reshape(length, local_width),
                d_key.reshape(length, local_width),
                d_value.reshape(length, local_width),
            ],
            axis=1,
        ).astype(jnp.bfloat16)
        grad_bq = jnp.stack(
            [
                jnp.sum(d_qkv[:, 0], axis=0, dtype=jnp.float32),
                jnp.sum(d_qkv[:, 2], axis=0, dtype=jnp.float32),
            ]
        )
        d_qkv = d_qkv.reshape(length, 3 * local_width)
        grad_wq = weight_grad(gathered_first, d_qkv).reshape(full_width, 3, local_width)
        d_normed = input_sum(d_qkv, qkv_weight)
        grad_now = grad_mid + norm_grad(residual, total_first, factor_first, d_normed, full_width)
        grad_terms = (grad_wq, grad_bq, grad_wo, grad_bo, grad_wu, grad_bu, grad_wd, grad_bd)
        collected.insert(0, grad_terms)
    stacked_wq = jnp.stack([member[0] for member in collected])
    stacked_bq = jnp.stack([member[1] for member in collected])
    stacked_wo = jnp.stack([member[2] for member in collected])
    stacked_bo = jnp.stack([member[3] for member in collected])
    stacked_wu = jnp.stack([member[4] for member in collected])
    stacked_bu = jnp.stack([member[5] for member in collected])
    stacked_wd = jnp.stack([member[6] for member in collected])
    stacked_bd = jnp.stack([member[7] for member in collected])
    (
        stacked_wq,
        stacked_bq,
        stacked_wo,
        stacked_bo,
        stacked_wu,
        stacked_bu,
        stacked_wd,
        stacked_bd,
    ) = lax.psum(
        (
            stacked_wq,
            stacked_bq,
            stacked_wo,
            stacked_bo,
            stacked_wu,
            stacked_bu,
            stacked_wd,
            stacked_bd,
        ),
        "dp",
    )
    grad_stream = grad_now * column_keep
    return (
        layer_outs[0],
        layer_outs[-1],
        grad_stream,
        stacked_wq,
        stacked_bq,
        stacked_wo,
        stacked_bo,
        stacked_wu,
        stacked_bu,
        stacked_wd,
        stacked_bd,
    )


def solution(mesh):
    in_specs = (
        P("dp", "mp"),
        P("dp"),
        P(None, None, None, "mp"),
        P(None, None, "mp"),
        P(None, "mp", None),
        P(None, "mp"),
        P(None, None, "mp"),
        P(None, "mp"),
        P(None, "mp", None),
        P(None, "mp"),
        P("dp", "mp"),
    )
    out_specs = (
        P("dp", "mp"),
        P("dp", "mp"),
        P("dp", "mp"),
        P(None, None, None, "mp"),
        P(None, None, "mp"),
        P(None, "mp", None),
        P(None, "mp"),
        P(None, None, "mp"),
        P(None, "mp"),
        P(None, "mp", None),
        P(None, "mp"),
    )
    return jax.shard_map(
        per_device, mesh=mesh, in_specs=in_specs, out_specs=out_specs, check_vma=False
    )
```

profile of v0, /device:TPU:0, one launch (start us, length us, event | category | flops | bytes accessed | tf_op | source)
XLA Modules:
  0.0 1572.1 jit_solution(15885857669364083318)
XLA Ops:
  9.0 20.5 %all-reduce.9 = (f32[2048]{0:T(1024)S(1)}, f32[2048]{0:T(1024)S(1)}) all-reduce(f32[2048]{0:T(1024)S(1)} %get-tuple-element.240, f32[2048]{0:T(1024)S(1)} %get-tuple-element.239), channel_id=1, replica_groups=mesh['dp'=8,'mp'=4] {'mp'}, use_global_device_ids=true, to_apply=%region_1.2 | all-reduce | flops 4096 | bytes 32768 | tf_op jit(solution)/shard_map/psum | solution.py:16
  35.9 58.6 %all-gather.9.cloned.1.call-done = bf16[2048,768]{0,1:T(8,128)(2,1)} async-done(((bf16[2048,192]{0,1:T(8,128)(2,1)}), bf16[2048,768]{0,1:T(8,128)(2,1)}) %all-gather.9.cloned.1.call-update) | async-done | bytes 3145744 | tf_op jit(solution)/shard_map/all_gather | solution.py:29
  130.7 58.4 %reduce-scatter.9.cloned.1.call-done = bf16[2048,192]{0,1:T(8,128)(2,1)} async-done(((bf16[2048,768]{0,1:T(8,128)(2,1)}), bf16[2048,192]{0,1:T(8,128)(2,1)}) %reduce-scatter.9.cloned.1.call-update) | async-done | bytes 786448 | tf_op jit(solution)/shard_map/reduce_scatter | solution.py:38
  190.9 18.0 %all-reduce.8 = (f32[2048]{0:T(1024)S(1)}, f32[2048]{0:T(1024)S(1)}) all-reduce(f32[2048]{0:T(1024)S(1)} %get-tuple-element.246, f32[2048]{0:T(1024)S(1)} %get-tuple-element.245), channel_id=1, replica_groups=mesh['dp'=8,'mp'=4] {'mp'}, use_global_device_ids=true, to_apply=%region_16.17 | all-reduce | flops 4096 | bytes 32768 | tf_op jit(solution)/shard_map/psum | solution.py:16
  211.2 61.4 %all-gather.11.cloned.1.call-done = bf16[2048,768]{0,1:T(8,128)(2,1)} async-done(((bf16[2048,192]{0,1:T(8,128)(2,1)}), bf16[2048,768]{0,1:T(8,128)(2,1)}) %all-gather.11.cloned.1.call-update) | async-done | bytes 3145744 | tf_op jit(solution)/shard_map/all_gather | solution.py:29
  286.2 57.9 %reduce-scatter.11.cloned.1.call-done = bf16[2048,192]{0,1:T(8,128)(2,1)} async-done(((bf16[2048,768]{0,1:T(8,128)(2,1)}), bf16[2048,192]{0,1:T(8,128)(2,1)}) %reduce-scatter.11.cloned.1.call-update) | async-done | bytes 786448 | tf_op jit(solution)/shard_map/reduce_scatter | solution.py:38
  345.7 17.8 %all-reduce.7 = (f32[2048]{0:T(1024)S(1)}, f32[2048]{0:T(1024)S(1)}) all-reduce(f32[2048]{0:T(1024)S(1)} %get-tuple-element.244, f32[2048]{0:T(1024)S(1)} %get-tuple-element.243), channel_id=1, replica_groups=mesh['dp'=8,'mp'=4] {'mp'}, use_global_device_ids=true, to_apply=%region_21.22 | all-reduce | flops 4096 | bytes 32768 | tf_op jit(solution)/shard_map/psum | solution.py:16
  365.9 61.3 %all-gather.13.cloned.1.call-done = bf16[2048,768]{0,1:T(8,128)(2,1)} async-done(((bf16[2048,192]{0,1:T(8,128)(2,1)}), bf16[2048,768]{0,1:T(8,128)(2,1)}) %all-gather.13.cloned.1.call-update) | async-done | bytes 3145744 | tf_op jit(solution)/shard_map/all_gather | solution.py:29
  466.1 59.0 %reduce-scatter.13.cloned.1.call-done = bf16[2048,192]{0,1:T(8,128)(2,1)} async-done(((bf16[2048,768]{0,1:T(8,128)(2,1)}), bf16[2048,192]{0,1:T(8,128)(2,1)}) %reduce-scatter.13.cloned.1.call-update) | async-done | bytes 786448 | tf_op jit(solution)/shard_map/reduce_scatter | solution.py:38
  528.9 18.7 %all-reduce.6 = (f32[2048]{0:T(1024)}, f32[2048]{0:T(1024)}) all-reduce(f32[2048]{0:T(1024)} %get-tuple-element.242, f32[2048]{0:T(1024)} %get-tuple-element.241), channel_id=1, replica_groups=mesh['dp'=8,'mp'=4] {'mp'}, use_global_device_ids=true, to_apply=%region_34.35 | all-reduce | flops 4096 | bytes 32768 | tf_op jit(solution)/shard_map/psum | solution.py:16
  554.9 57.9 %all-gather.15.cloned.1.call-done = bf16[2048,768]{0,1:T(8,128)(2,1)} async-done(((bf16[2048,192]{0,1:T(8,128)(2,1)}), bf16[2048,768]{0,1:T(8,128)(2,1)}) %all-gather.15.cloned.1.call-update) | async-done | bytes 3145744 | tf_op jit(solution)/shard_map/all_gather | solution.py:29
  612.8 7.6 fusion.188
  620.4 56.7 %all-gather.17.cloned.1.call-done = bf16[2048,768]{0,1:T(8,128)(2,1)} async-done(((bf16[2048,192]{0,1:T(8,128)(2,1)}), bf16[2048,768]{0,1:T(8,128)(2,1)}) %all-gather.17.cloned.1.call-update) | async-done | bytes 3145744 | tf_op jit(solution)/shard_map/all_gather | solution.py:47
  677.1 10.1 convert_reduce_fusion
  692.9 7.9 convolution_convert_fusion.2
  701.0 51.0 %reduce-scatter.17.cloned.1.call-done = bf16[2048,192]{0,1:T(8,128)(2,1)} async-done(((bf16[2048,768]{0,1:T(8,128)(2,1)}), bf16[2048,192]{0,1:T(8,128)(2,1)}) %reduce-scatter.17.cloned.1.call-update) | async-done | bytes 786448 | tf_op jit(solution)/shard_map/reduce_scatter | solution.py:51
  754.4 11.5 psum.148
  767.2 47.9 %reduce-scatter.15.cloned.1.call-done = bf16[2048,192]{0,1:T(8,128)(2,1)} async-done(((bf16[2048,768]{0,1:T(8,128)(2,1)}), bf16[2048,192]{0,1:T(8,128)(2,1)}) %reduce-scatter.15.cloned.1.call-update) | async-done | bytes 786448 | tf_op jit(solution)/shard_map/reduce_scatter | solution.py:38
  824.9 59.4 %all-gather.19.cloned.1.call-done = bf16[2048,768]{0,1:T(8,128)(2,1)} async-done(((bf16[2048,192]{0,1:T(8,128)(2,1)}), bf16[2048,768]{0,1:T(8,128)(2,1)}) %all-gather.19.cloned.1.call-update) | async-done | bytes 3145744 | tf_op jit(solution)/shard_map/all_gather | solution.py:47
  930.9 6.7 multiply_convert_fusion.1
  947.4 59.0 %reduce-scatter.19.cloned.1.call-done = bf16[2048,192]{0,1:T(8,128)(2,1)} async-done(((bf16[2048,768]{0,1:T(8,128)(2,1)}), bf16[2048,192]{0,1:T(8,128)(2,1)}) %reduce-scatter.19.cloned.1.call-update) | async-done | bytes 786448 | tf_op jit(solution)/shard_map/reduce_scatter | solution.py:51
  1007.8 10.6 psum.149
  1021.6 62.0 %all-gather.21.cloned.1.call-done = bf16[2048,768]{0,1:T(8,128)(2,1)} async-done(((bf16[2048,192]{0,1:T(8,128)(2,1)}), bf16[2048,768]{0,1:T(8,128)(2,1)}) %all-gather.21.cloned.1.call-update) | async-done | bytes 3145744 | tf_op jit(solution)/shard_map/all_gather | solution.py:47
  1083.6 10.1 convert_reduce_fusion.1
  1099.5 59.0 %reduce-scatter.21.cloned.1.call-done = bf16[2048,192]{0,1:T(8,128)(2,1)} async-done(((bf16[2048,768]{0,1:T(8,128)(2,1)}), bf16[2048,192]{0,1:T(8,128)(2,1)}) %reduce-scatter.21.cloned.1.call-update) | async-done | bytes 786448 | tf_op jit(solution)/shard_map/reduce_scatter | solution.py:51
  1159.8 10.6 psum.150
  1176.9 60.5 %all-gather.23.cloned.1.call-done = bf16[2048,768]{0,1:T(8,128)(2,1)} async-done(((bf16[2048,192]{0,1:T(8,128)(2,1)}), bf16[2048,768]{0,1:T(8,128)(2,1)}) %all-gather.23.cloned.1.call-update) | async-done | bytes 3145744 | tf_op jit(solution)/shard_map/all_gather | solution.py:47
  1283.4 6.7 multiply_convert_fusion
  1306.7 7.1 convolution_bitcast_fusion
  1343.2 24.9 %all-reduce.4 = (f32[2,2,192]{2,1,0:T(2,128)}, f32[2,192]{1,0:T(2,128)}, f32[2,768]{1,0:T(2,128)}, f32[2,192]{1,0:T(2,128)}) all-reduce(f32[2,2,192]{2,1,0:T(2,128)S(1)} %pad_maximum_fusion.9, f32[2,192]{1,0:T(2,128)S(1)} %pad_maximum_fusion.10, f32[2,768]{1,0:T(2,128)S(1)} %pad_maximum_fusion.8, ...), channel_id=1, replica_groups=mesh['dp'=8,'mp'=4] {'dp'}, use_global_device_ids=true, to_apply=%region_63.64 | all-reduce | flops 3072 | bytes 24576 | tf_op jit(solution)/shard_map/psum | solution.py:313
  1369.7 10.3 psum.151
  1382.8 171.5 %all-reduce.12.cloned.1.call-done = (f32[2,768,3,192]{1,3,2,0:T(8,128)}, f32[2,192,768]{2,1,0:T(8,128)}, f32[2,768,768]{2,1,0:T(8,128)}, f32[2,768,768]{2,1,0:T(8,128)}) async-done(((f32[2,768,3,192]{1,3,2,0:T(8,128)}, f32[2,192,768]{2,1,0:T(8,128)}, f32[2,768,768]{2,1,0:T(8,128)}, f32[2,768,768]{2,1,0:T(8,128)}), (f32[2,768,3,192]{1,3,2,0:T(8,128)}, f32[2,192,768]{2,1,0:T(8,128)}, ...) | async-done | bytes 14155792 | tf_op jit(solution)/shard_map/psum | solution.py:313
  (651 shorter events, 314.6 us)
Async XLA Ops:
  7.2 87.3 %all-gather.9.cloned.1.call-start = ((), (), s32[]{:S(2)}) async-start(), calls=%async_computation.8 | async-start | bytes 3932160 | tf_op jit(solution)/shard_map/all_gather | solution.py:29
  7.3 336.8 %copy-start.124 = (f32[192]{0:T(256)}, f32[192]{0:T(256)S(1)}, u32[]{:S(2)}) copy-start(f32[192]{0:T(256)S(1)} %compare_convert_fusion) | copy-start | bytes 2308
  32.6 156.6 %reduce-scatter.9.cloned.1.call-start = ((), (), s32[]{:S(2)}) async-start(), calls=%async_computation.9 | async-start | bytes 3932160 | tf_op jit(solution)/shard_map/reduce_scatter | solution.py:38
  32.8 88.0 %copy-start.127 = (f32[3,64]{1,0:T(4,128)}, f32[3,64]{1,0:T(4,128)S(1)}, u32[]{:S(2)}) copy-start(f32[3,64]{1,0:T(4,128)S(1)} %add.479) | copy-start | bytes 2308
  35.1 81.1 %copy-start.74 = (pred[512,2048]{1,0:T(8,128)(4,1)}, pred[512,2048]{1,0:T(8,128)(4,1)S(1)}, u32[]{:S(2)}) copy-start(pred[512,2048]{1,0:T(8,128)(4,1)S(1)} %fusion.42) | copy-start | bytes 3145732
  35.9 72.3 %copy-start.25 = (pred[512,1536]{1,0:T(8,128)(4,1)}, pred[512,1536]{1,0:T(8,128)(4,1)S(1)}, u32[]{:S(2)}) copy-start(pred[512,1536]{1,0:T(8,128)(4,1)S(1)} %compare_and_fusion) | copy-start | bytes 2359300
  130.1 142.5 %all-gather.11.cloned.1.call-start = ((), (), s32[]{:S(2)}) async-start(), calls=%async_computation.10 | async-start | bytes 3932160 | tf_op jit(solution)/shard_map/all_gather | solution.py:29
  190.9 153.2 %copy-start.10 = (f32[2048,192]{0,1:T(8,128)}, f32[2048,192]{0,1:T(8,128)S(1)}, u32[]{:S(2)}) copy-start(f32[2048,192]{0,1:T(8,128)S(1)} %get-tuple-element.279) | copy-start | bytes 4718596
  210.6 133.5 %reduce-scatter.11.cloned.1.call-start = ((), (), s32[]{:S(2)}) async-start(), calls=%async_computation.11 | async-start | bytes 3932160 | tf_op jit(solution)/shard_map/reduce_scatter | solution.py:38
  285.0 142.2 %all-gather.13.cloned.1.call-start = ((), (), s32[]{:S(2)}) async-start(), calls=%async_computation.12 | async-start | bytes 3932160 | tf_op jit(solution)/shard_map/all_gather | solution.py:29
  345.7 85.5 %copy-start.8 = (f32[2048,192]{0,1:T(8,128)}, f32[2048,192]{0,1:T(8,128)S(1)}, u32[]{:S(2)}) copy-start(f32[2048,192]{0,1:T(8,128)S(1)} %get-tuple-element.352) | copy-start | bytes 4718596
  345.7 81.5 %copy-start.56 = (bf16[2,768,3,192]{1,3,2,0:T(8,128)(2,1)S(1)}, bf16[2,768,3,192]{1,3,2,0:T(8,128)(2,1)}, u32[]{:S(2)}) copy-start(bf16[2,768,3,192]{1,3,2,0:T(8,128)(2,1)} %param.53) | copy-start | bytes 5308420
  365.1 160.0 %reduce-scatter.13.cloned.1.call-start = ((), (), s32[]{:S(2)}) async-start(), calls=%async_computation.13 | async-start | bytes 3932160 | tf_op jit(solution)/shard_map/reduce_scatter | solution.py:38
  466.0 146.8 %all-gather.15.cloned.1.call-start = ((), (), s32[]{:S(2)}) async-start(), calls=%async_computation.14 | async-start | bytes 3932160 | tf_op jit(solution)/shard_map/all_gather | solution.py:29
  550.8 126.4 %all-gather.17.cloned.1.call-start = ((), (), s32[]{:S(2)}) async-start(), calls=%async_computation.16 | async-start | bytes 3932160 | tf_op jit(solution)/shard_map/all_gather | solution.py:47
  554.9 197.1 %reduce-scatter.17.cloned.1.call-start = ((), (), s32[]{:S(2)}) async-start(), calls=%async_computation.17 | async-start | bytes 3932160 | tf_op jit(solution)/shard_map/reduce_scatter | solution.py:51
  692.9 122.2 %reduce-scatter.15.cloned.1.call-start = ((), (), s32[]{:S(2)}) async-start(), calls=%async_computation.15 | async-start | bytes 3932160 | tf_op jit(solution)/shard_map/reduce_scatter | solution.py:38
  700.9 183.3 %all-gather.19.cloned.1.call-start = ((), (), s32[]{:S(2)}) async-start(), calls=%async_computation.18 | async-start | bytes 3932160 | tf_op jit(solution)/shard_map/all_gather | solution.py:47
  820.5 186.0 %reduce-scatter.19.cloned.1.call-start = ((), (), s32[]{:S(2)}) async-start(), calls=%async_computation.19 | async-start | bytes 3932160 | tf_op jit(solution)/shard_map/reduce_scatter | solution.py:51
  947.3 71.1 %copy-start.111 = (f32[2048]{0:T(1024)S(1)}, f32[2048]{0:T(1024)}, u32[]{:S(2)}) copy-start(f32[2048]{0:T(1024)} %copy-done.110) | copy-start | bytes 24580
  947.3 71.1 %copy-start.156 = (f32[2048]{0:T(1024)S(1)}, f32[2048]{0:T(1024)}, u32[]{:S(2)}) copy-start(f32[2048]{0:T(1024)} %copy-done.155) | copy-start | bytes 24580
  947.3 71.1 %copy-start.14 = (f32[2048,192]{0,1:T(8,128)S(1)}, f32[2048,192]{0,1:T(8,128)}, u32[]{:S(2)}) copy-start(f32[2048,192]{0,1:T(8,128)} %get-tuple-element.276) | copy-start | bytes 4718596
  947.4 71.1 %copy-start.103 = (f32[2048]{0:T(1024)S(1)}, f32[2048]{0:T(1024)}, u32[]{:S(2)}) copy-start(f32[2048]{0:T(1024)} %copy-done.102) | copy-start | bytes 24580
  947.4 71.1 %copy-start.158 = (bf16[192]{0:T(256)(128)(2,1)S(1)}, bf16[192]{0:T(256)(128)(2,1)}, u32[]{:S(2)}) copy-start(bf16[192]{0:T(256)(128)(2,1)} %copy-done.157) | copy-start | bytes 1156
  947.4 136.2 %all-gather.21.cloned.1.call-start = ((), (), s32[]{:S(2)}) async-start(), calls=%async_computation.20 | async-start | bytes 3932160 | tf_op jit(solution)/shard_map/all_gather | solution.py:47
  1007.8 75.8 %copy-start.165 = (f32[768]{0:T(1024)S(1)}, f32[768]{0:T(1024)}, u32[]{:S(2)}) copy-start(f32[768]{0:T(1024)} %copy-done.164) | copy-start | bytes 9220
  1021.6 136.9 %reduce-scatter.21.cloned.1.call-start = ((), (), s32[]{:S(2)}) async-start(), calls=%async_computation.21 | async-start | bytes 3932160 | tf_op jit(solution)/shard_map/reduce_scatter | solution.py:51
  1099.4 71.0 %copy-start.109 = (f32[2048]{0:T(1024)S(1)}, f32[2048]{0:T(1024)}, u32[]{:S(2)}) copy-start(f32[2048]{0:T(1024)} %copy-done.108) | copy-start | bytes 24580
  1099.4 71.1 %copy-start.144 = (f32[2048]{0:T(1024)S(1)}, f32[2048]{0:T(1024)}, u32[]{:S(2)}) copy-start(f32[2048]{0:T(1024)} %copy-done.143) | copy-start | bytes 24580
  1099.4 138.0 %all-gather.23.cloned.1.call-start = ((), (), s32[]{:S(2)}) async-start(), calls=%async_computation.22 | async-start | bytes 3932160 | tf_op jit(solution)/shard_map/all_gather | solution.py:47
  1175.4 192.7 %reduce-scatter.23.cloned.1.call-start = ((), (), s32[]{:S(2)}) async-start(), calls=%async_computation.23 | async-start | bytes 3932160 | tf_op jit(solution)/shard_map/reduce_scatter | solution.py:51
  1299.5 254.8 %all-reduce.12.cloned.1.call-start = ((), (), s32[]{:S(2)}) async-start(), calls=%async_computation.24 | async-start | bytes 28311552 | tf_op jit(solution)/shard_map/psum | solution.py:313
  (195 other events, 1864.8 us)
Sparse Core Ops, SparseCore 0:
  32.7 61.7 all-gather.8
  130.2 58.8 reduce-scatter.8
  210.7 61.8 all-gather.10
  285.2 58.8 reduce-scatter.10
  365.3 61.8 all-gather.12
  466.2 58.8 reduce-scatter.12
  550.9 61.8 all-gather.14
  614.9 62.1 all-gather.16
  693.0 58.8 reduce-scatter.16
  754.7 60.3 reduce-scatter.14
  820.6 63.5 all-gather.18
  947.5 58.8 reduce-scatter.18
  1021.7 61.8 all-gather.20
  1099.6 58.8 reduce-scatter.20
  1175.5 61.8 all-gather.22
  1299.7 58.8 reduce-scatter.22
  1363.6 190.6 all-reduce.11
where the time goes:
time: 1580 us; the launch traced here: 1570 us
  waiting for transfers between devices  1040 us (66%)
  matrix products  201 us (13%)
  blocking collectives  143 us (9%)
  other arithmetic  111 us (7%)
  local copies, waits for them, and re-layouts  57.1 us (4%)
  between operations  16.8 us (1%)
    all_gather x4, waiting for transfers between devices, project_in(): gathered = lax.all_gather(normed, 'mp', axis=1, tiled=True)  239 us
    all_gather x4, waiting for transfers between devices, branch_spread(): return lax.all_gather(grad_rows, 'mp', axis=1, tiled=True)  239 us
    reduce_scatter x4, waiting for transfers between devices, branch_sum(): lax.psum_scatter(jnp.dot(local_rows, weight, preferred_element_type=jnp.f...  223 us
    psum x1, waiting for transfers between devices, per_device(): lax.psum((stacked_wq, stacked_bq, stacked_wo, stacked_bo, stacked_wu, sta...  171 us
    reduce_scatter x4, waiting for transfers between devices, input_sum(): lax.psum_scatter(lax.dot_general(grad_rows, weight, CONTRACT_COLS, prefer...  169 us
    psum x4, blocking collectives, norm_stats(): lax.psum((jnp.sum(stream_now, axis=1), jnp.sum(stream_now * stream_now, a...  75 us
    unnamed x424, local copies, waits for them, and re-layouts  47.5 us
    psum x4, blocking collectives, norm_grad(): inner_sum = lax.psum(jnp.sum(d_normed * stream_now, axis=1), 'mp')  43.1 us
  transfers between devices with their start and end apart: 17, of which 16 were waited for; matrix products, arithmetic and copies ran while one was open for 5% of the time, Pallas kernels for 0%

commit v1 on v0

v1 whole, which is shorter than its diff:
```python
import functools

import jax
import jax.numpy as jnp
from jax import lax
from jax.experimental import pallas as pl
from jax.experimental.pallas import tpu as pltpu
from jax.sharding import Mesh, PartitionSpec as P

HEADS = 12
EPS = 1e-06
ROWS_T = (((0,), (0,)), ((), ()))
COLS_T = (((1,), (1,)), ((), ()))
NEG = -1e30
AXES = ("g", "p", "c", "mp")
PIECES = 4
bf16 = jnp.bfloat16
f32 = jnp.float32


def dot_nt(a, b):
    return lax.dot_general(a, b, COLS_T, preferred_element_type=f32)


def dot_tn(a, b):
    return lax.dot_general(a, b, ROWS_T, preferred_element_type=f32)


def dot_nn(a, b):
    return jnp.dot(a, b, preferred_element_type=f32)


def lane_mask(head, half):
    lanes = lax.broadcasted_iota(jnp.int32, (1, 2 * half), 1)
    return (lanes < half) if head == 0 else (lanes >= half)


def pick(mask, values):
    return jnp.where(mask, values, jnp.zeros_like(values))


def fwd_block(q, k, v, half, diagonal):
    out = None
    highs = []
    sums = []
    for head in (0, 1):
        mask = lane_mask(head, half)
        scores = dot_nt(q, pick(mask, k))
        if diagonal:
            rows = lax.broadcasted_iota(jnp.int32, scores.shape, 0)
            cols = lax.broadcasted_iota(jnp.int32, scores.shape, 1)
            scores = jnp.where(rows >= cols, scores, NEG)
        high = jnp.max(scores, axis=1, keepdims=True)
        chance = jnp.exp(scores - high)
        sums.append(jnp.sum(chance, axis=1, keepdims=True))
        highs.append(high)
        part = dot_nn(chance.astype(bf16), pick(mask, v))
        out = part if out is None else out + part
    first = lane_mask(0, half)
    shape = out.shape
    high = jnp.where(first, jnp.broadcast_to(highs[0], shape), jnp.broadcast_to(highs[1], shape))
    total = jnp.where(first, jnp.broadcast_to(sums[0], shape), jnp.broadcast_to(sums[1], shape))
    return out, high, total


def merge_into(acc_ref, high_ref, sum_ref, rows, part):
    out, high, total = part
    old = high_ref[rows, :]
    new = jnp.maximum(old, high)
    keep = jnp.exp(old - new)
    take = jnp.exp(high - new)
    acc_ref[rows, :] = acc_ref[rows, :] * keep + out * take
    sum_ref[rows, :] = sum_ref[rows, :] * keep + total * take
    high_ref[rows, :] = new


def fwd_local_kernel(quarter, half, s_ref, q_ref, k_ref, v_ref, acc_ref, high_ref, sum_ref):
    for i in (0, 1):
        rows = pl.ds(i * quarter, quarter)
        out, high, total = fwd_block(q_ref[rows, :], k_ref[rows, :], v_ref[rows, :], half, True)
        acc_ref[rows, :] = out
        high_ref[rows, :] = high
        sum_ref[rows, :] = total

    @pl.when(s_ref[0] > 0)
    def _():
        early = pl.ds(0, quarter)
        late = pl.ds(quarter, quarter)
        part = fwd_block(q_ref[late, :], k_ref[early, :], v_ref[early, :], half, False)
        merge_into(acc_ref, high_ref, sum_ref, late, part)


def fwd_remote_kernel(
    quarter, half, s_ref, q_ref, k_ref, v_ref, acc_in, high_in, sum_in, out_ref, lse_ref, acc_ref, high_ref, sum_ref
):
    acc_ref[...] = acc_in[...]
    high_ref[...] = high_in[...]
    sum_ref[...] = sum_in[...]

    @pl.when(s_ref[0] > 0)
    def _():
        early = pl.ds(0, quarter)
        late = pl.ds(quarter, quarter)
        part = fwd_block(q_ref[late, :], k_ref[early, :], v_ref[early, :], half, False)
        merge_into(acc_ref, high_ref, sum_ref, late, part)
        which = pl.ds(pl.multiple_of(s_ref[1] * quarter, quarter), quarter)
        part = fwd_block(q_ref[which, :], k_ref[which, :], v_ref[which, :], half, False)
        merge_into(acc_ref, high_ref, sum_ref, which, part)

    total = sum_ref[...]
    out_ref[...] = (acc_ref[...] / total).astype(out_ref.dtype)
    lse = high_ref[...] + jnp.log(total)
    flat = lse.T
    lse_ref[0, 0:1, :] = flat[0:1, :]
    lse_ref[0, 1:2, :] = flat[half : half + 1, :]


def bwd_block(q, do, k, v, lse, inner, half, diagonal):
    k_t = k.T
    d_key = d_value = d_query_t = None
    subl = lax.broadcasted_iota(jnp.int32, (2 * half, 1), 0)
    for head in (0, 1):
        mask = lane_mask(head, half)
        scores = dot_nt(pick(mask, k), q)
        chance = jnp.exp(scores - lse[head : head + 1, :])
        if diagonal:
            keys = lax.broadcasted_iota(jnp.int32, scores.shape, 0)
            queries = lax.broadcasted_iota(jnp.int32, scores.shape, 1)
            chance = jnp.where(queries >= keys, chance, 0.0)
        d_chance = dot_nt(pick(mask, v), do)
        d_scores = (chance * (d_chance - inner[head : head + 1, :])).astype(bf16)
        part_v = dot_nn(chance.astype(bf16), pick(mask, do))
        part_k = dot_nn(d_scores, pick(mask, q))
        row_mask = (subl < half) if head == 0 else (subl >= half)
        part_q = dot_nn(pick(row_mask, k_t), d_scores)
        d_value = part_v if d_value is None else d_value + part_v
        d_key = part_k if d_key is None else d_key + part_k
        d_query_t = part_q if d_query_t is None else d_query_t + part_q
    return d_query_t, d_key, d_value


def bwd_remote_kernel(
    quarter, half, s_ref, q_ref, k_ref, v_ref, o_ref, do_ref, lse_ref, dqt_ref, dk_ref, dv_ref, inner_ref, ak_ref, av_ref
):
    flat = (o_ref[...].astype(f32) * do_ref[...].astype(f32)).T
    inner_ref[0, 0:1, :] = jnp.sum(flat[:half, :], axis=0, keepdims=True)
    inner_ref[0, 1:2, :] = jnp.sum(flat[half:, :], axis=0, keepdims=True)
    dqt_ref[...] = jnp.zeros_like(dqt_ref)
    ak_ref[...] = jnp.zeros_like(ak_ref)
    av_ref[...] = jnp.zeros_like(av_ref)

    @pl.when(s_ref[0] > 0)
    def _():
        def job(q_rows, k_rows):
            dqt, dk, dv = bwd_block(
                q_ref[q_rows, :],
                do_ref[q_rows, :],
                k_ref[k_rows, :],
                v_ref[k_rows, :],
                lse_ref[0, 0:2, q_rows],
                inner_ref[0, 0:2, q_rows],
                half,
                False,
            )
            dqt_ref[0, :, q_rows] += dqt
            ak_ref[k_rows, :] += dk
            av_ref[k_rows, :] += dv

        job(pl.ds(quarter, quarter), pl.ds(0, quarter))
        which = pl.ds(pl.multiple_of(s_ref[1] * quarter, quarter), quarter)
        job(which, which)

    dk_ref[...] = ak_ref[...].astype(dk_ref.dtype)
    dv_ref[...] = av_ref[...].astype(dv_ref.dtype)


def bwd_local_kernel(
    quarter, half, scale, s_ref, q_ref, k_ref, v_ref, do_ref, lse_ref, inner_ref, dqt_in, dq_ref, dk_ref, dv_ref, dqt_ref, ak_ref, av_ref
):
    for i in (0, 1):
        rows = pl.ds(i * quarter, quarter)
        dqt, dk, dv = bwd_block(
            q_ref[rows, :], do_ref[rows, :], k_ref[rows, :], v_ref[rows, :],
            lse_ref[0, 0:2, rows], inner_ref[0, 0:2, rows], half, True,
        )
        dqt_ref[:, rows] = dqt_in[0, :, rows] + dqt
        ak_ref[rows, :] = dk
        av_ref[rows, :] = dv

    @pl.when(s_ref[0] > 0)
    def _():
        early = pl.ds(0, quarter)
        late = pl.ds(quarter, quarter)
        dqt, dk, dv = bwd_block(
            q_ref[late, :], do_ref[late, :], k_ref[early, :], v_ref[early, :],
            lse_ref[0, 0:2, late], inner_ref[0, 0:2, late], half, False,
        )
        dqt_ref[:, late] += dqt
        ak_ref[early, :] += dk
        av_ref[early, :] += dv

    dq_ref[...] = (dqt_ref[...].T * scale).astype(dq_ref.dtype)
    dk_ref[...] = ak_ref[...].astype(dk_ref.dtype)
    dv_ref[...] = av_ref[...].astype(dv_ref.dtype)


class Attention:
    def __init__(self, tokens, heads, size):
        self.tokens, self.pairs, self.size = tokens, heads // 2, size
        self.quarter = tokens // 2
        self.width = 2 * size

    def rows(self, first):
        return pl.BlockSpec((self.tokens, self.width), lambda j, s: (0, first + j))

    def flat(self):
        return pl.BlockSpec((1, 8, self.tokens), lambda j, s: (j, 0, 0))

    def turned(self):
        return pl.BlockSpec((1, self.width, self.tokens), lambda j, s: (j, 0, 0))

    def call(self, kernel, in_specs, out_specs, out_shape, scratch, blocks, dots):
        flops = blocks * dots * 2 * self.quarter * self.quarter * self.width * 2 * self.pairs
        return pl.pallas_call(
            kernel,
            out_shape=out_shape,
            grid_spec=pltpu.PrefetchScalarGridSpec(
                num_scalar_prefetch=1,
                grid=(self.pairs,),
                in_specs=in_specs,
                out_specs=out_specs,
                scratch_shapes=scratch,
            ),
            compiler_params=pltpu.CompilerParams(vmem_limit_bytes=40 * 2**20),
            cost_estimate=pl.CostEstimate(
                flops=flops * 2, bytes_accessed=8 * 2**20, transcendentals=blocks * 2 * self.pairs * self.quarter**2
            ),
        )

    def shape(self, dtype):
        return jax.ShapeDtypeStruct((self.tokens, self.pairs * self.width), dtype)

    def flat_shape(self):
        return jax.ShapeDtypeStruct((self.pairs, 8, self.tokens), f32)

    def scratch(self):
        return pltpu.VMEM((self.tokens, self.width), f32)

    def forward_local(self, flags, qkv):
        n = self.pairs
        return self.call(
            functools.partial(fwd_local_kernel, self.quarter, self.size),
            [self.rows(0), self.rows(n), self.rows(2 * n)],
            [self.rows(0)] * 3,
            [self.shape(f32)] * 3,
            [],
            3,
            2,
        )(flags, qkv, qkv, qkv)

    def forward_remote(self, flags, qkv, kv, acc, high, total):
        n = self.pairs
        return self.call(
            functools.partial(fwd_remote_kernel, self.quarter, self.size),
            [self.rows(0), self.rows(0), self.rows(n), self.rows(0), self.rows(0), self.rows(0)],
            [self.rows(0), self.flat()],
            [self.shape(bf16), self.flat_shape()],
            [self.scratch()] * 3,
            2,
            2,
        )(flags, qkv, kv, kv, acc, high, total)

    def backward_remote(self, flags, qkv, kv, out, d_out, lse):
        n = self.pairs
        return self.call(
            functools.partial(bwd_remote_kernel, self.quarter, self.size),
            [self.rows(0), self.rows(0), self.rows(n), self.rows(0), self.rows(0), self.flat()],
            [self.turned(), self.rows(0), self.rows(0), self.flat()],
            [
                jax.ShapeDtypeStruct((n, self.width, self.tokens), f32),
                self.shape(bf16),
                self.shape(bf16),
                self.flat_shape(),
            ],
            [self.scratch()] * 2,
            2,
            5,
        )(flags, qkv, kv, kv, out, d_out, lse)

    def backward_local(self, flags, qkv, d_out, lse, inner, dqt):
        n = self.pairs
        return self.call(
            functools.partial(bwd_local_kernel, self.quarter, self.size, float(self.size) ** -0.5),
            [self.rows(0), self.rows(n), self.rows(2 * n), self.rows(0), self.flat(), self.flat(), self.turned()],
            [self.rows(0)] * 3,
            [self.shape(bf16)] * 3,
            [pltpu.VMEM((self.width, self.tokens), f32), self.scratch(), self.scratch()],
            3,
            5,
        )(flags, qkv, qkv, qkv, d_out, lse, inner, dqt)


class Moves:
    def __init__(self, groups, pieces, chips):
        self.sizes = (groups, pieces, 2, chips)
        self.c = lax.axis_index("c")
        self.z = lax.axis_index("mp")
        self.spot = 2 * (self.z % 2) + self.c

    def permute(self, value, target):
        groups, pieces, cores, chips = self.sizes
        place = lambda g, p, c, z: ((g * pieces + p) * cores + c) * chips + z
        pairs = [
            (place(g, p, c, z), place(*target(g, p, c, z)))
            for g in range(groups)
            for p in range(pieces)
            for c in range(cores)
            for z in range(chips)
        ]
        return lax.ppermute(value, AXES, pairs)

    def core(self, value):
        return self.permute(value, lambda g, p, c, z: (g, p, 1 - c, z))

    def chip(self, value, bit):
        return self.permute(value, lambda g, p, c, z: (g, p, c, z ^ bit))

    def column(self, value, bit):
        return self.permute(value, lambda g, p, c, z: (g, p ^ bit, c, z))

    def both_cores(self, mine, axis=0):
        other = self.core(mine)
        return self.in_order(mine, other, axis)

    def in_order(self, mine, other, axis=0):
        return jnp.where(
            self.c == 0,
            jnp.concatenate([mine, other], axis=axis),
            jnp.concatenate([other, mine], axis=axis),
        )

    @staticmethod
    def shuffle(blocks, index):
        odd = (index % 2) == 1
        high = index >= 2
        blocks = [jnp.where(odd, blocks[j ^ 1], blocks[j]) for j in range(4)]
        return [jnp.where(high, blocks[j ^ 2], blocks[j]) for j in range(4)]

    def to_rows(self, block):
        quarter = block.shape[0] // 4
        got = []
        for k in range(4):
            spot = self.z ^ k
            which = jnp.where(spot == 0, 0, jnp.where(spot == 1, 3, spot - 1))
            send = lax.dynamic_slice_in_dim(block, which * quarter, quarter, 0).astype(bf16)

            def target(g, p, c, z, k=k):
                t = z ^ k
                return (g, p, t % 2, 2 * c + t // 2)

            got.append(self.permute(send, target))
        return jnp.concatenate(self.shuffle(got, self.spot), axis=1)

    def to_columns(self, rows):
        width = rows.shape[1] // 4
        blocks = [rows[:, j * width : (j + 1) * width].astype(bf16) for j in range(4)]
        blocks = self.shuffle(blocks, self.spot)
        got = []
        for k in range(4):

            def target(g, p, c, z, k=k):
                t = 2 * (z % 2) + c
                return (g, p, z // 2, t ^ k)

            got.append(self.permute(blocks[k], target))
        parts = self.shuffle(got, self.z)
        return jnp.concatenate([parts[0], parts[2], parts[3], parts[1]], axis=0).astype(f32)


def norm(stream):
    total = jnp.sum(stream, axis=1, keepdims=True)
    squares = jnp.sum(stream * stream, axis=1, keepdims=True)
    factor = lax.rsqrt((squares + total * total) / stream.shape[1] + EPS)
    return total, factor, (stream * factor).astype(bf16)


def norm_back(stream, total, factor, d_normed):
    inner = jnp.sum(d_normed * stream, axis=1, keepdims=True)
    term = factor * factor * factor * inner / stream.shape[1]
    return factor * d_normed - term * (stream + total)


def gelu_parts(x):
    a = 0.7978845608028654
    t = jnp.tanh(a * (x + 0.044715 * (x * x * x)))
    value = 0.5 * x * (1.0 + t)
    slope = 0.5 * (1.0 + t) + 0.5 * x * (1.0 - t * t) * (a * (1.0 + 3 * 0.044715 * (x * x)))
    return value.astype(bf16), slope.astype(bf16)


def per_device(stream, seq_lens, w_qkv, b_qv, w_out, b_out, w_up, b_up, w_down, b_down, cotangent):
    groups = lax.axis_size("g")
    mv = Moves(groups, lax.axis_size("p"), lax.axis_size("mp"))
    c, z = mv.c, mv.z
    piece = lax.axis_index("p") * 2 + c
    length, local = stream.shape
    chips = lax.axis_size("mp")
    width = local * chips
    layers = w_qkv.shape[0]
    hidden = w_up.shape[2]
    size = width // HEADS
    quarter = length // 4
    tokens = 2 * quarter
    att = Attention(tokens, HEADS // 2, size)
    keep = (jnp.arange(width, dtype=jnp.int32) < width - 1).astype(f32)[None, :]
    keep16 = keep.astype(bf16)
    step = hidden // (2 * PIECES)
    part = local // (2 * PIECES)

    lens_other = mv.core(seq_lens)
    lens = jnp.where(c == z // 2, seq_lens, lens_other)
    flags = jnp.stack([(lens[0] > quarter).astype(jnp.int32), 1 - z % 2])

    flat = jnp.concatenate([b_qv.reshape(-1), b_out.reshape(-1), b_up.reshape(-1), b_down.reshape(-1)])[None]
    other = mv.chip(flat, 1)
    pair = jnp.where(z % 2 == 0, jnp.concatenate([flat, other]), jnp.concatenate([other, flat]))
    other = mv.chip(pair, 2)
    biases = jnp.where(z < 2, jnp.concatenate([pair, other]), jnp.concatenate([other, pair]))
    cuts = [0, layers * 2 * local, layers * local, layers * hidden, layers * local]
    ends = [sum(cuts[: i + 1]) for i in range(5)]

    def bias(i, shape):
        return biases[:, ends[i] : ends[i + 1]].reshape((chips,) + shape)

    all_qv = bias(0, (layers, 2, local))
    all_qv = lax.dynamic_slice_in_dim(all_qv, 2 * c, 2, 0)
    bias_qv = jnp.transpose(all_qv, (1, 2, 0, 3)).reshape(layers, 2, 2 * local)
    bias_out = jnp.transpose(bias(1, (layers, local)), (1, 0, 2)).reshape(layers, width)
    bias_down = jnp.transpose(bias(3, (layers, local)), (1, 0, 2)).reshape(layers, width)
    all_up = bias(2, (layers, PIECES, 2, step))
    all_up = lax.dynamic_index_in_dim(all_up, c, 3, keepdims=False)
    bias_up = jnp.transpose(all_up, (1, 2, 0, 3)).reshape(layers, chips * PIECES * step)

    def gather_heads(kinds):
        count = kinds.shape[0]
        cut = kinds.reshape(count, PIECES, 2, part, width)
        mine = lax.dynamic_index_in_dim(cut, c, 2, keepdims=False).reshape(count * PIECES * part, width)
        every = lax.all_gather(mine, "mp", axis=0, tiled=True).reshape(2, 2, count, PIECES, part, width)
        got = mv.core(lax.dynamic_index_in_dim(every, 1 - c, 0, keepdims=False))
        own = lax.dynamic_index_in_dim(every, c, 0, keepdims=False)
        whole = mv.in_order(own[:, :, :, None], got[:, :, :, None], axis=3)
        return jnp.transpose(whole, (1, 0, 2, 3, 4, 5)).reshape(count, 2 * local, width)

    def gather_units(rows):
        return lax.all_gather(lax.all_gather(rows, "mp", axis=0, tiled=True), "p", axis=0, tiled=True)

    def turned_qkv(layer):
        return jnp.transpose(w_qkv[layer], (1, 2, 0))

    qkv_rows, out_rows, up_rows, down_rows = [], [], [], []
    for layer in range(layers):
        if layer == 0:
            qkv_rows.append(gather_heads(turned_qkv(layer)).reshape(6 * local, width))
            out_rows.append(gather_heads(w_out[layer][None])[0])
        else:
            both = gather_heads(jnp.concatenate([turned_qkv(layer), w_out[layer][None]]))
            qkv_rows.append(both[:3].reshape(6 * local, width))
            out_rows.append(both[3])
        up_rows.append(gather_units(lax.dynamic_slice_in_dim(w_up[layer], piece * step, step, 1).T))
        down_rows.append(gather_units(lax.dynamic_slice_in_dim(w_down[layer], piece * step, step, 0)))

    x = mv.both_cores(mv.to_rows(stream)).astype(f32) * keep
    saved = []
    outs = []
    half_heads = 2 * local
    for layer in range(layers):
        total, factor, n = norm(x)
        n_mine = lax.dynamic_slice_in_dim(n, c * quarter, quarter, 0)
        n_far = mv.both_cores(mv.chip(n_mine, 1))
        scale = float(size) ** -0.5
        proj = dot_nt(n, qkv_rows[layer])
        zero = jnp.zeros((half_heads,), f32)
        add = jnp.concatenate([bias_qv[layer, 0], zero, bias_qv[layer, 1]])
        mult = jnp.concatenate([zero + scale, zero + 1.0, zero + 1.0])
        qkv = ((proj + add).astype(bf16).astype(f32) * mult).astype(bf16)
        acc, high, sums = att.forward_local(flags, qkv)
        kv = (dot_nt(n_far, qkv_rows[layer][half_heads:]) + add[half_heads:]).astype(bf16)
        o, lse = att.forward_remote(flags, qkv, kv, acc, high, sums)
        branch = dot_nn(o, out_rows[layer]).astype(bf16)
        branch = branch.astype(f32) + mv.core(branch).astype(f32)
        x1 = x + (branch + bias_out[layer]) * keep
        total1, factor1, n1 = norm(x1)
        g, slope = gelu_parts(dot_nt(n1, up_rows[layer]) + bias_up[layer])
        branch = dot_nn(g, down_rows[layer]).astype(bf16)
        branch = branch.astype(f32) + mv.core(branch).astype(f32)
        saved.append((x, total, factor, n, n_far, qkv, kv, o, lse, x1, total1, factor1, n1, g, slope))
        x = x1 + (branch + bias_down[layer]) * keep
        outs.append(lax.dynamic_slice_in_dim(x, c * quarter, quarter, 0))

    def finish_sum(value):
        value = lax.psum_scatter(value, "mp", scatter_dimension=0, tiled=True)
        if groups > 1:
            value = lax.psum(value, "g")
        return lax.all_gather(value, ("p", "c"), axis=0, tiled=True)

    def sum_units(rows):
        return finish_sum(lax.psum_scatter(rows.astype(bf16), "p", scatter_dimension=0, tiled=True)).astype(f32)

    def sum_heads(kinds):
        count = kinds.shape[0]
        cut = kinds.astype(bf16).reshape(count, 2, PIECES, 2, part, width)
        mine = lax.dynamic_index_in_dim(cut, c, 3, keepdims=False)
        got = mv.core(lax.dynamic_index_in_dim(cut, 1 - c, 3, keepdims=False))
        whole = mv.in_order(mine, got, axis=1)
        whole = jnp.transpose(whole, (2, 1, 0, 3, 4)).reshape(-1, width)
        done = finish_sum(lax.psum_scatter(whole, "p", scatter_dimension=0, tiled=True))
        done = jnp.transpose(done.reshape(PIECES, 2, count, part, width), (2, 0, 1, 3, 4))
        return done.reshape(count, local, width).astype(f32)

    dx = mv.both_cores(mv.to_rows(cotangent)).astype(f32)
    late = None
    gw_qkv, gw_out, gw_up, gw_down = {}, {}, {}, {}
    gb_qv, gb_out, gb_up, gb_down = {}, {}, {}, {}
    for layer in reversed(range(layers)):
        x, total, factor, n, n_far, qkv, kv, o, lse, x1, total1, factor1, n1, g, slope = saved[layer]
        dm = dx.astype(bf16) * keep16
        gb_down[layer] = jnp.sum(dm, axis=0, dtype=f32)
        gw_down[layer] = sum_units(dot_tn(g, dm))
        dh = (dot_nt(dm, down_rows[layer]) * slope.astype(f32)).astype(bf16)
        gb_up[layer] = jnp.sum(dh, axis=0, dtype=f32)
        gw_up[layer] = sum_units(dot_tn(dh, n1)).T
        dn1 = dot_nn(dh, up_rows[layer]).astype(bf16)
        dn1 = dn1.astype(f32) + mv.core(dn1).astype(f32)
        dx1 = dx + norm_back(x1, total1, factor1, dn1)
        da = dx1.astype(bf16) * keep16
        gb_out[layer] = jnp.sum(da, axis=0, dtype=f32)
        g_out = dot_tn(o, da)
        do = dot_nt(da, out_rows[layer]).astype(bf16)
        dqt, dkr, dvr, inner = att.backward_remote(flags, qkv, kv, o, do, lse)
        dkv = jnp.concatenate([dkr, dvr], axis=1)
        far = dot_nn(dkv, qkv_rows[layer][half_heads:]).astype(bf16)
        far_got = mv.core(lax.dynamic_slice_in_dim(far, (1 - c) * quarter, quarter, 0))
        far_mine = lax.dynamic_slice_in_dim(far, c * quarter, quarter, 0)
        far_sum = (far_mine.astype(f32) + far_got.astype(f32)).astype(bf16)
        back = mv.chip(far_sum, 1)
        dq, dk, dv = att.backward_local(flags, qkv, do, lse, inner, dqt)
        dqkv = jnp.concatenate([dq, dk, dv], axis=1)
        gb_qv[layer] = jnp.stack(
            [
                jnp.sum(dq, axis=0, dtype=f32),
                jnp.sum(dv, axis=0, dtype=f32) + jnp.sum(dvr, axis=0, dtype=f32),
            ]
        )
        g_qkv = jnp.concatenate(
            [dot_tn(dq, n), dot_tn(dkv, n_far) + dot_tn(dqkv[:, half_heads:], n)]
        ).reshape(3, half_heads, width)
        if layer > 0:
            late = jnp.concatenate([g_qkv, g_out[None]])
            if layer > 1:
                late = None
                done = sum_heads(jnp.concatenate([g_qkv, g_out[None]]))
                gw_qkv[layer], gw_out[layer] = done[:3], done[3]
            else:
                held = late
        else:
            if layers > 1:
                done = sum_heads(jnp.concatenate([held, g_out[None]]))
                gw_qkv[1], gw_out[1], gw_out[0] = done[:3], done[3], done[4]
                gw_qkv[0] = sum_heads(g_qkv)
            else:
                done = sum_heads(jnp.concatenate([g_qkv, g_out[None]]))
                gw_qkv[0], gw_out[0] = done[:3], done[3]
        dn = dot_nn(dqkv, qkv_rows[layer])
        zero_rows = jnp.zeros_like(back)
        wide = jnp.where(
            c == 0, jnp.concatenate([back, zero_rows]), jnp.concatenate([zero_rows, back])
        )
        dn = (dn + wide.astype(f32)).astype(bf16)
        dn = dn.astype(f32) + mv.core(dn).astype(f32)
        dx = dx1 + norm_back(x, total, factor, dn)

    grad_stream = mv.to_columns(lax.dynamic_slice_in_dim(dx * keep, c * quarter, quarter, 0))
    outs = [mv.to_columns(value) for value in outs]

    once = (c == 0).astype(f32)

    def by_chip(value):
        return jnp.transpose(value.reshape(layers, chips, local) * once, (1, 0, 2)).reshape(chips, -1)

    qv = jnp.stack([gb_qv[i] for i in range(layers)]).reshape(layers, 2, 2, local)
    qv = jnp.transpose(qv, (2, 0, 1, 3)).reshape(2, -1)
    none = jnp.zeros_like(qv)
    qv = jnp.where(c == 0, jnp.concatenate([qv, none]), jnp.concatenate([none, qv]))
    up = jnp.stack([gb_up[i] for i in range(layers)]).reshape(layers, PIECES, chips, step)
    up = jnp.transpose(up, (2, 0, 1, 3))[:, :, :, None]
    none = jnp.zeros_like(up)
    up = jnp.where(c == 0, jnp.concatenate([up, none], axis=3), jnp.concatenate([none, up], axis=3))
    flat = jnp.concatenate(
        [
            qv,
            by_chip(jnp.stack([gb_out[i] for i in range(layers)])),
            up.reshape(chips, -1),
            by_chip(jnp.stack([gb_down[i] for i in range(layers)])),
        ],
        axis=1,
    )
    flat = flat + mv.core(flat)
    flat = flat + mv.column(flat, 1)
    flat = flat + mv.column(flat, 2)
    flat = flat + mv.chip(flat, 1)
    flat = flat + mv.chip(flat, 2)
    if groups > 1:
        flat = lax.psum(flat, "g")
    flat = lax.dynamic_index_in_dim(flat, z, 0, keepdims=False)
    pieces = [flat[ends[i] : ends[i + 1]] for i in range(4)]
    every = range(layers)
    return (
        outs[0],
        outs[-1],
        grad_stream,
        jnp.stack([jnp.transpose(gw_qkv[i], (2, 0, 1)) for i in every]),
        pieces[0].reshape(layers, 2, local),
        jnp.stack([gw_out[i] for i in every]),
        pieces[1].reshape(layers, local),
        jnp.stack([gw_up[i] for i in every]),
        pieces[2].reshape(layers, hidden),
        jnp.stack([gw_down[i] for i in every]),
        pieces[3].reshape(layers, local),
    )


def solution(mesh):
    rows, chips = mesh.shape["dp"], mesh.shape["mp"]
    grid = Mesh(mesh.devices.reshape(rows // (2 * PIECES), PIECES, 2, chips), AXES)
    dp = ("g", "p", "c")
    in_specs = (
        P(dp, "mp"),
        P(dp),
        P(None, None, None, "mp"),
        P(None, None, "mp"),
        P(None, "mp", None),
        P(None, "mp"),
        P(None, None, "mp"),
        P(None, "mp"),
        P(None, "mp", None),
        P(None, "mp"),
        P(dp, "mp"),
    )
    out_specs = (
        P(dp, "mp"),
        P(dp, "mp"),
        P(dp, "mp"),
        P(None, None, None, "mp"),
        P(None, None, "mp"),
        P(None, "mp", None),
        P(None, "mp"),
        P(None, None, "mp"),
        P(None, "mp"),
        P(None, "mp", None),
        P(None, "mp"),
    )
    return jax.shard_map(per_device, mesh=grid, in_specs=in_specs, out_specs=out_specs, check_vma=False)
```

time: 1580 us -> 951 us (0.60)
  waiting for transfers between devices: 1040 us -> 321 us
  Pallas kernels: 0 us -> 92.8 us
  matrix products: 201 us -> 133 us
  starting transfers between devices: 1.47 us -> 64.8 us
    all_gather x8 -> x11, waiting for transfers between devices: 478 us -> 54.8 us  [the longest x5 54.7 us: finish_sum(): return lax.all_gather(value, ('p', 'c'), axis=0, tiled=True)]
    reduce_scatter x8 -> x12, waiting for transfers between devices: 392 us -> 174 us  [the longest x2 80.7 us: sum_heads(): lax.psum_scatter(whole, 'p', scatter_dimension=0, tiled=True)]
    psum x1 -> x0, waiting for transfers between devices: 171 us -> none  [per_device(): lax.psum((stacked_wq, stacked_bq, stacked_wo, stacked_bo, stacked_wu, sta...]
    psum x9 -> x0, blocking collectives: 143 us -> none  [the longest x4 75 us: norm_stats(): lax.psum((jnp.sum(stream_now, axis=1), jnp.sum(stream_now * stream_now, a...]
    all_gather x0 -> x6, blocking collectives: none -> 142 us  [the longest x4 104 us: gather_units(): lax.all_gather(rows, 'mp', axis=0, tiled=True)]
    pallas_call x0 -> x8, Pallas kernels: none -> 92.8 us  [the longest x2 29.3 us: backward_local(): self.call(functools.partial(bwd_local_kernel, self.quarter, self.size, fl...]
    ppermute x0 -> x51, waiting for transfers between devices: none -> 89.9 us  [permute(): return lax.ppermute(value, AXES, pairs)]
    dot_general x72 -> x32, matrix products: 201 us -> 133 us  [the longest x10 51.4 us: dot_nt(): return lax.dot_general(a, b, COLS_T, preferred_element_type=f32)]
  transfers between devices with their start and end apart: 17 -> 74, of which waited for: 16 -> 27; matrix products, arithmetic and copies ran while one was open for 5% -> 26% of each run, Pallas kernels for 0% -> 9%
where the time goes in v1:
time: 951 us; the launch traced here: 947 us
  waiting for transfers between devices  321 us (34%)
  blocking collectives  142 us (15%)
  matrix products  133 us (14%)
  other arithmetic  118 us (12%)
  Pallas kernels  92.8 us (10%)
  starting transfers between devices  64.8 us (7%)
  local copies, waits for them, and re-layouts  58.7 us (6%)
  between operations  16.7 us (2%)
    all_gather x4, blocking collectives, gather_units(): lax.all_gather(rows, 'mp', axis=0, tiled=True)  104 us
    ppermute x51, waiting for transfers between devices, permute(): return lax.ppermute(value, AXES, pairs)  89.9 us
    reduce_scatter x2, waiting for transfers between devices, sum_heads(): lax.psum_scatter(whole, 'p', scatter_dimension=0, tiled=True)  80.7 us
    reduce_scatter x6, waiting for transfers between devices, finish_sum(): value = lax.psum_scatter(value, 'mp', scatter_dimension=0, tiled=True)  63.2 us
    ppermute x51, starting transfers between devices, permute(): return lax.ppermute(value, AXES, pairs)  62.6 us
    all_gather x5, waiting for transfers between devices, finish_sum(): return lax.all_gather(value, ('p', 'c'), axis=0, tiled=True)  54.7 us
    dot_general x10, matrix products, dot_nt(): return lax.dot_general(a, b, COLS_T, preferred_element_type=f32)  51.4 us
    dot_general x10, matrix products, dot_nn(): return jnp.dot(a, b, preferred_element_type=f32)  41.2 us
  transfers between devices with their start and end apart: 74, of which 27 were waited for; matrix products, arithmetic and copies ran while one was open for 26% of the time, Pallas kernels for 9%

profile of v1, /device:TPU:0, one launch (start us, length us, event | category | flops | bytes accessed | tf_op | source)
XLA Modules:
  0.0 946.6 jit_solution(17380340013795206436)
XLA Ops:
  13.6 24.3 %all_gather.53 = bf16[384,768]{1,0:T(8,128)(2,1)} all-gather(bf16[96,768]{1,0:T(8,128)(2,1)} %bitcast.223), channel_id=1, replica_groups=mesh['g'=1,'p'=4,'c'=2,'mp'=4] {'mp'}, dimensions={0}, use_global_device_ids=true | all-gather | bytes 737280 | tf_op jit(solution)/shard_map/all_gather | solution.py:455
  39.2 24.2 %all-gather = bf16[1,384,768]{2,1,0:T(8,128)(2,1)} all-gather(bf16[1,96,768]{2,1,0:T(8,128)(2,1)S(1)} %constant_dynamic-slice_fusion.10), channel_id=2, replica_groups=mesh['g'=1,'p'=4,'c'=2,'mp'=4] {'mp'}, dimensions={1}, use_global_device_ids=true | all-gather | bytes 737280 | tf_op jit(solution)/shard_map/all_gather | solution.py:455
  84.1 16.7 %all_gather.52 = bf16[384,768]{1,0:T(8,128)(2,1)S(1)} all-gather(bf16[96,768]{1,0:T(8,128)(2,1)S(1)} %bitcast.222), channel_id=1, replica_groups=mesh['g'=1,'p'=4,'c'=2,'mp'=4] {'mp'}, dimensions={0}, use_global_device_ids=true | all-gather | bytes 737280 | tf_op jit(solution)/shard_map/all_gather | solution.py:448
  102.9 10.3 %convert_multiply_fusion = (f32[1024,768]{0,1:T(8,128)}, bf16[1024,768]{0,1:T(8,128)(2,1)S(1)}) fusion(f32[768]{0:T(1024)S(1)} %fusion.77, bf16[512,192]{0,1:T(8,128)(2,1)S(1)} %get-tuple-element.202, bf16[512,192]{0,1:T(8,128)(2,1)S(1)} %get-tuple-element.201, bf16[512,192]{0,1:T(8,128)(2,1)S(1)} %get-tuple-element.200, ...), kind=kLoop, calls=%fused_computation.67 | loop fusion | flops 18087936 | bytes 6294529 | tf_op jit(solution)/shard_map/mul | solution.py:472
  123.1 13.1 %collective-permute-done.9 = bf16[512,768]{0,1:T(8,128)(2,1)} collective-permute-done((bf16[512,768]{0,1:T(8,128)(2,1)S(1)}, bf16[512,768]{0,1:T(8,128)(2,1)}, u32[]{:S(2)}, u32[]{:S(2)}) %collective-permute-start.9) | collective-permute-done | bytes 786464 | tf_op jit(solution)/shard_map/ppermute | solution.py:320
  147.6 12.0 %shard_map.194 = (f32[1024,384]{1,0:T(8,128)S(1)}, f32[1024,384]{1,0:T(8,128)S(1)}, f32[1024,384]{1,0:T(8,128)S(1)}) custom-call(s32[2]{0:T(128)S(1)} %pad_add_fusion.s_ref, bf16[1024,1152]{1,0:T(8,128)(2,1)S(1)} %multiply_convert_fusion.5.q_ref.k_ref.v_ref, bf16[1024,1152]{1,0:T(8,128)(2,1)S(1)} %multiply_convert_fusion.5.q_ref.k_ref.v_ref, ...), custom_call_target="tpu_custom_call" | custom-call | flops 4831838208 | bytes 8388608 | tf_op jit(solution)/shard_map/pallas_call | solution.py:251
  159.6 9.0 shard_map.195
  171.3 24.1 %all_gather.58 = bf16[384,768]{1,0:T(8,128)(2,1)} all-gather(bf16[96,768]{1,0:T(8,128)(2,1)S(1)} %bitcast.224), channel_id=1, replica_groups=mesh['g'=1,'p'=4,'c'=2,'mp'=4] {'mp'}, dimensions={0}, use_global_device_ids=true | all-gather | bytes 737280 | tf_op jit(solution)/shard_map/all_gather | solution.py:455
  228.1 31.4 %all-gather.2 = bf16[1,384,768]{2,1,0:T(8,128)(2,1)} all-gather(bf16[1,96,768]{2,1,0:T(8,128)(2,1)S(1)} %constant_dynamic-slice_fusion.6), channel_id=4, replica_groups=mesh['g'=1,'p'=4,'c'=2,'mp'=4] {'mp'}, dimensions={1}, use_global_device_ids=true | all-gather | bytes 737280 | tf_op jit(solution)/shard_map/all_gather | solution.py:455
  268.2 11.7 %shard_map.196 = (f32[1024,384]{1,0:T(8,128)S(1)}, f32[1024,384]{1,0:T(8,128)S(1)}, f32[1024,384]{1,0:T(8,128)S(1)}) custom-call(s32[2]{0:T(128)S(1)} %pad_add_fusion.s_ref, bf16[1024,1152]{1,0:T(8,128)(2,1)S(1)} %multiply_convert_fusion.4.q_ref.k_ref.v_ref, bf16[1024,1152]{1,0:T(8,128)(2,1)S(1)} %multiply_convert_fusion.4.q_ref.k_ref.v_ref, ...), custom_call_target="tpu_custom_call" | custom-call | flops 4831838208 | bytes 8388608 | tf_op jit(solution)/shard_map/pallas_call | solution.py:251
  283.1 9.0 shard_map.197
  321.3 7.9 fusion.63
  329.3 13.4 %convert_reduce_fusion = (f32[1536]{0:T(1024)}, bf16[1024,1536]{1,0:T(8,128)(2,1)S(1)}) fusion(f32[1024,1536]{1,0:T(8,128)} %fusion.63, f32[1536]{0:T(1024)} %add.537, bf16[1,1536,768]{2,1,0:T(8,128)(2,1)} %all-gather.36.cloned.1.call-done, bf16[768]{0:T(1024)(128)(2,1)} %fusion.78, bf16[512,192]{0,1:T(8,128)(2,1)} %copy-done.34, ...), kind=kOutput, calls=%fused_computation.22 | convolution fusion | flops 2471754240 | bytes 13383169 | tf_op jit(solution)/shard_map/dot_general | solution.py:22
  353.9 10.7 %convert_reduce_fusion.4 = (f32[768]{0:T(1024)}, bf16[1024,768]{0,1:T(8,128)(2,1)S(1)}) fusion(bf16[768]{0:T(1024)(128)(2,1)S(1)} %copy-done.86, f32[1024,768]{0,1:T(8,128)S(1)} %copy-done.17, f32[1024]{0:T(1024)S(1)} %get-tuple-element.114, f32[1024]{0:T(1024)S(1)} %fusion.70, bf16[1024,768]{0,1:T(8,128)(2,1)} %collective-permute-done.32, ...), kind=kLoop, calls=%fused_computation.39 | loop fusion | flops 29097216 | bytes 9454081 | tf_op jit(solution)/shard_map/reduce_sum | solution.py:536
  366.9 10.9 %shard_map.198 = (f32[3,128,1024]{2,1,0:T(8,128)S(1)}, bf16[1024,384]{1,0:T(8,128)(2,1)S(1)}, bf16[1024,384]{1,0:T(8,128)(2,1)S(1)}, f32[3,8,1024]{2,1,0:T(8,128)S(1)}) custom-call(s32[2]{0:T(128)S(1)} %pad_add_fusion.s_ref, bf16[1024,1152]{1,0:T(8,128)(2,1)S(1)} %copy-done.8, bf16[1024,768]{1,0:T(8,128)(2,1)S(1)} %add_convert_fusion.4.k_ref.v_ref, ...), custom_call_target="tpu_custom_call" | custom-call | flops 8053063680 | bytes 8388608 | tf_op jit(solution)/shard_map/pallas_call | solution.py:275
  386.3 14.4 %shard_map.199 = (bf16[1024,384]{1,0:T(8,128)(2,1)S(1)}, bf16[1024,384]{1,0:T(8,128)(2,1)S(1)}, bf16[1024,384]{1,0:T(8,128)(2,1)S(1)}) custom-call(s32[2]{0:T(128)S(1)} %pad_add_fusion.s_ref, bf16[1024,1152]{1,0:T(8,128)(2,1)S(1)} %copy-done.8, bf16[1024,1152]{1,0:T(8,128)(2,1)S(1)} %copy-done.8, bf16[1024,1152]{1,0:T(8,128)(2,1)S(1)} %copy-done.8, ...), custom_call_target="tpu_custom_call" | custom-call | flops 12079595520 | bytes 8388608 | tf_op jit(solution)/shard_map/pallas_call | solution.py:292
  417.0 10.2 %convert_reduce_fusion.3 = (f32[768]{0:T(1024)}, bf16[1024,768]{0,1:T(8,128)(2,1)S(1)}, f32[1024,768]{0,1:T(8,128)}) fusion(bf16[768]{0:T(1024)(128)(2,1)S(1)} %copy-done.87, f32[1024,768]{0,1:T(8,128)S(1)} %copy-done.16, f32[1024]{0:T(1024)S(1)} %copy-done.77, f32[1024]{0:T(1024)S(1)} %fusion.72, bf16[1024,768]{0,1:T(8,128)(2,1)} %collective-permute-done.35, ...), kind=kLoop, calls=%fused_computation.38 | loop fusion | flops 35388672 | bytes 18903552 | tf_op jit(solution)/shard_map/reduce_sum | solution.py:527
  440.5 9.4 convolution_convert_fusion
  476.6 13.7 %convert_reduce_fusion.5 = (f32[768]{0:T(1024)S(1)}, bf16[1024,768]{0,1:T(8,128)(2,1)S(1)}, f32[1024,768]{0,1:T(8,128)}, f32[768]{0:T(1024)S(1)}) fusion(bf16[768]{0:T(1024)(128)(2,1)S(1)} %copy-done.88, f32[1024,768]{0,1:T(8,128)S(1)} %copy-done.25, f32[1024,768]{0,1:T(8,128)S(1)} %copy-done.22, f32[1024]{0:T(1024)S(1)} %copy-done.75, f32[1024]{0:T(1024)S(1)} %fusion.74, ...), kind=kLoop, calls=%fused_computation.40 | loop fusion | flops 31455744 | bytes 15748609 | tf_op jit(solution)/shard_map/reduce_sum | solution.py:536
  500.9 10.9 %shard_map.200 = (f32[3,128,1024]{2,1,0:T(8,128)S(1)}, bf16[1024,384]{1,0:T(8,128)(2,1)S(1)}, bf16[1024,384]{1,0:T(8,128)(2,1)S(1)}, f32[3,8,1024]{2,1,0:T(8,128)S(1)}) custom-call(s32[2]{0:T(128)S(1)} %pad_add_fusion.s_ref, bf16[1024,1152]{1,0:T(8,128)(2,1)S(1)} %copy-done.6, bf16[1024,768]{1,0:T(8,128)(2,1)S(1)} %copy-done.10, ...), custom_call_target="tpu_custom_call" | custom-call | flops 8053063680 | bytes 8388608 | tf_op jit(solution)/shard_map/pallas_call | solution.py:275
  512.1 14.9 %shard_map.201 = (bf16[1024,384]{1,0:T(8,128)(2,1)S(1)}, bf16[1024,384]{1,0:T(8,128)(2,1)S(1)}, bf16[1024,384]{1,0:T(8,128)(2,1)S(1)}) custom-call(s32[2]{0:T(128)S(1)} %pad_add_fusion.s_ref, bf16[1024,1152]{1,0:T(8,128)(2,1)S(1)} %copy-done.6, bf16[1024,1152]{1,0:T(8,128)(2,1)S(1)} %copy-done.6, bf16[1024,1152]{1,0:T(8,128)(2,1)S(1)} %copy-done.6, ...), custom_call_target="tpu_custom_call" | custom-call | flops 12079595520 | bytes 8388608 | tf_op jit(solution)/shard_map/pallas_call | solution.py:292
  539.1 30.0 %reduce-scatter.29.cloned.1.call-done = bf16[384,768]{1,0:T(8,128)(2,1)} async-done(((bf16[1536,768]{1,0:T(8,128)(2,1)}), bf16[384,768]{1,0:T(8,128)(2,1)}) %reduce-scatter.29.cloned.1.call-update) | async-done | bytes 589840 | tf_op jit(solution)/shard_map/reduce_scatter | solution.py:507
  569.1 45.4 %reduce-scatter.17.cloned.1.call-done = bf16[480,768]{1,0:T(8,128)(2,1)} async-done(((bf16[1920,768]{1,0:T(8,128)(2,1)}), bf16[480,768]{1,0:T(8,128)(2,1)}) %reduce-scatter.17.cloned.1.call-update) | async-done | bytes 737296 | tf_op jit(solution)/shard_map/reduce_scatter | solution.py:516
  614.6 35.3 %reduce-scatter.13.cloned.1.call-done = bf16[288,768]{1,0:T(8,128)(2,1)} async-done(((bf16[1152,768]{1,0:T(8,128)(2,1)}), bf16[288,768]{1,0:T(8,128)(2,1)}) %reduce-scatter.13.cloned.1.call-update) | async-done | bytes 442384 | tf_op jit(solution)/shard_map/reduce_scatter | solution.py:516
  649.9 24.3 %reduce-scatter.27.cloned.1.call-done = bf16[96,768]{1,0:T(8,128)(2,1)} async-done(((bf16[384,768]{1,0:T(8,128)(2,1)}), bf16[96,768]{1,0:T(8,128)(2,1)}) %reduce-scatter.27.cloned.1.call-update) | async-done | bytes 147472 | tf_op jit(solution)/shard_map/reduce_scatter | solution.py:501
  674.3 22.5 %reduce-scatter.23.cloned.1.call-done = bf16[96,768]{1,0:T(8,128)(2,1)} async-done(((bf16[384,768]{1,0:T(8,128)(2,1)}), bf16[96,768]{1,0:T(8,128)(2,1)}) %reduce-scatter.23.cloned.1.call-update) | async-done | bytes 147472 | tf_op jit(solution)/shard_map/reduce_scatter | solution.py:501
  702.7 16.5 %reduce-scatter.35.cloned.1.call-done = bf16[96,768]{1,0:T(8,128)(2,1)} async-done(((bf16[384,768]{1,0:T(8,128)(2,1)}), bf16[96,768]{1,0:T(8,128)(2,1)}) %reduce-scatter.35.cloned.1.call-update) | async-done | bytes 147472 | tf_op jit(solution)/shard_map/reduce_scatter | solution.py:501
  743.4 34.7 %collective-permute-done.14 = bf16[512,192]{0,1:T(8,128)(2,1)S(1)} collective-permute-done((bf16[512,192]{0,1:T(8,128)(2,1)}, bf16[512,192]{0,1:T(8,128)(2,1)S(1)}, u32[]{:S(2)}, u32[]{:S(2)}) %collective-permute-start.14) | collective-permute-done | bytes 196640 | tf_op jit(solution)/shard_map/ppermute | solution.py:320
  788.5 8.0 fusion.42
  844.0 21.4 %all_gather.62 = bf16[576,768]{1,0:T(8,128)(2,1)S(1)} all-gather(bf16[72,768]{1,0:T(8,128)(2,1)} %reduce-scatter.15.cloned.1.call-done), channel_id=1, replica_groups=mesh['g'=1,'p'=4,'c'=2,'mp'=4] {'p','c'}, dimensions={0}, use_global_device_ids=true | all-gather | bytes 995328 | tf_op jit(solution)/shard_map/all_gather | solution.py:504
  881.2 26.1 %all-gather.30.cloned.1.call-done = bf16[768,768]{1,0:T(8,128)(2,1)} async-done(((bf16[96,768]{1,0:T(8,128)(2,1)}), bf16[768,768]{1,0:T(8,128)(2,1)}) %all-gather.30.cloned.1.call-update) | async-done | bytes 1179664 | tf_op jit(solution)/shard_map/all_gather | solution.py:504
  911.5 23.2 %all-gather.24.cloned.1.call-done = bf16[960,768]{1,0:T(8,128)(2,1)} async-done(((bf16[120,768]{1,0:T(8,128)(2,1)}), bf16[960,768]{1,0:T(8,128)(2,1)}) %all-gather.24.cloned.1.call-update) | async-done | bytes 1474576 | tf_op jit(solution)/shard_map/all_gather | solution.py:504
  (610 shorter events, 340.5 us)
Async XLA Ops:
  7.2 113.4 %all-gather.16.cloned.1.call-start = ((), (), s32[]{:S(2)}) async-start(), calls=%async_computation.12 | async-start | bytes 2211840 | tf_op jit(solution)/shard_map/all_gather | solution.py:448
  11.7 189.0 %all-gather.18.cloned.1.call-start = ((), (), s32[]{:S(2)}) async-start(), calls=%async_computation.13 | async-start | bytes 2949120 | tf_op jit(solution)/shard_map/all_gather | solution.py:455
  37.9 170.3 %all-gather.34.cloned.1.call-start = ((), (), s32[]{:S(2)}) async-start(), calls=%async_computation.33 | async-start | bytes 2949120 | tf_op jit(solution)/shard_map/all_gather | solution.py:455
  63.4 153.3 %all-gather.20.cloned.1.call-start = ((), (), s32[]{:S(2)}) async-start(), calls=%async_computation.14 | async-start | bytes 2949120 | tf_op jit(solution)/shard_map/all_gather | solution.py:448
  63.5 53.0 %collective-permute-start.5 = (s32[4]{0:T(128)S(1)}, s32[4]{0:T(128)S(1)}, u32[]{:S(2)}, u32[]{:S(2)}) collective-permute-start(s32[4]{0:T(128)S(1)} %copy-done.105), channel_id=1, source_target_pairs={{0,4},{1,5},{2,6},{3,7},{4,0},{5,1},{6,2},{7,3},{8,12},{9,13},{10,... | collective-permute-start | bytes 56 | tf_op jit(solution)/shard_map/ppermute | solution.py:320
  71.9 44.6 %collective-permute-start.7 = (f32[1,3072]{1,0:T(1,128)}, f32[1,3072]{1,0:T(1,128)}, u32[]{:S(2)}, u32[]{:S(2)}) collective-permute-start(f32[1,3072]{1,0:T(1,128)} %bitcast.11), channel_id=1, source_target_pairs={{0,1},{1,0},{2,3},{3,2},{4,5},{5,4},{6,7},{7,6},{8,9},{9,8},{10,11... | collective-permute-start | bytes 36872 | tf_op jit(solution)/shard_map/ppermute | solution.py:320
  102.5 218.9 %all-gather.22.cloned.1.call-start = ((), (), s32[]{:S(2)}) async-start(), calls=%async_computation.15 | async-start | bytes 2949120 | tf_op jit(solution)/shard_map/all_gather | solution.py:455
  195.4 133.9 %all-gather.36.cloned.1.call-start = ((), (), s32[]{:S(2)}) async-start(), calls=%async_computation.34 | async-start | bytes 2949120 | tf_op jit(solution)/shard_map/all_gather | solution.py:455
  220.1 39.5 %collective-permute-start.18 = (bf16[2,4,4,24,768]{4,3,2,1,0:T(8,128)(2,1)}, bf16[2,4,4,24,768]{4,3,2,1,0:T(8,128)(2,1)}, u32[]{:S(2)}, u32[]{:S(2)}) collective-permute-start(bf16[2,4,4,24,768]{4,3,2,1,0:T(8,128)(2,1)} %get-tuple-element.156), channel_id=1, source_target_pairs={{0,4},{1,5},{2,6},{3,7},{4,0},{5,1},{6,2},{7,3},{8,12},{9,13},{10,... | collective-permute-start | bytes 3538952 | tf_op jit(solution)/shard_map/ppermute | solution.py:320
  226.1 38.6 %collective-permute-start.19 = (bf16[512,768]{0,1:T(8,128)(2,1)}, bf16[512,768]{0,1:T(8,128)(2,1)}, u32[]{:S(2)}, u32[]{:S(2)}) collective-permute-start(bf16[512,768]{0,1:T(8,128)(2,1)} %constant_dynamic-slice_fusion.8), channel_id=1, source_target_pairs={{0,1},{1,0},{2,3},{3,2},{4,5},{5,4},{6,7},{7,6},{8,9},{9,8},{10,11... | collective-permute-start | bytes 2359304 | tf_op jit(solution)/shard_map/ppermute | solution.py:320
  259.6 277.6 %reduce-scatter.25.cloned.1.call-start = ((), (), s32[]{:S(2)}) async-start(), calls=%async_computation.24 | async-start | bytes 2949120 | tf_op jit(solution)/shard_map/reduce_scatter | solution.py:507
  412.2 125.7 %reduce-scatter.21.cloned.1.call-start = ((), (), s32[]{:S(2)}) async-start(), calls=%async_computation.21 | async-start | bytes 2949120 | tf_op jit(solution)/shard_map/reduce_scatter | solution.py:507
  439.9 98.7 %reduce-scatter.33.cloned.1.call-start = ((), (), s32[]{:S(2)}) async-start(), calls=%async_computation.30 | async-start | bytes 2949120 | tf_op jit(solution)/shard_map/reduce_scatter | solution.py:507
  449.9 119.1 %reduce-scatter.29.cloned.1.call-start = ((), (), s32[]{:S(2)}) async-start(), calls=%async_computation.27 | async-start | bytes 2949120 | tf_op jit(solution)/shard_map/reduce_scatter | solution.py:507
  467.4 147.1 %reduce-scatter.17.cloned.1.call-start = ((), (), s32[]{:S(2)}) async-start(), calls=%async_computation.18 | async-start | bytes 3686400 | tf_op jit(solution)/shard_map/reduce_scatter | solution.py:516
  497.1 152.8 %reduce-scatter.13.cloned.1.call-start = ((), (), s32[]{:S(2)}) async-start(), calls=%async_computation.16 | async-start | bytes 2211840 | tf_op jit(solution)/shard_map/reduce_scatter | solution.py:516
  537.1 137.1 %reduce-scatter.27.cloned.1.call-start = ((), (), s32[]{:S(2)}) async-start(), calls=%async_computation.25 | async-start | bytes 737280 | tf_op jit(solution)/shard_map/reduce_scatter | solution.py:501
  537.9 158.9 %reduce-scatter.23.cloned.1.call-start = ((), (), s32[]{:S(2)}) async-start(), calls=%async_computation.22 | async-start | bytes 737280 | tf_op jit(solution)/shard_map/reduce_scatter | solution.py:501
  538.5 180.7 %reduce-scatter.35.cloned.1.call-start = ((), (), s32[]{:S(2)}) async-start(), calls=%async_computation.31 | async-start | bytes 737280 | tf_op jit(solution)/shard_map/reduce_scatter | solution.py:501
  539.0 249.1 %reduce-scatter.31.cloned.1.call-start = ((), (), s32[]{:S(2)}) async-start(), calls=%async_computation.28 | async-start | bytes 737280 | tf_op jit(solution)/shard_map/reduce_scatter | solution.py:501
  569.1 242.0 %reduce-scatter.19.cloned.1.call-start = ((), (), s32[]{:S(2)}) async-start(), calls=%async_computation.19 | async-start | bytes 921600 | tf_op jit(solution)/shard_map/reduce_scatter | solution.py:501
  614.5 229.5 %reduce-scatter.15.cloned.1.call-start = ((), (), s32[]{:S(2)}) async-start(), calls=%async_computation.17 | async-start | bytes 552960 | tf_op jit(solution)/shard_map/reduce_scatter | solution.py:501
  649.9 215.8 %all-gather.28.cloned.1.call-start = ((), (), s32[]{:S(2)}) async-start(), calls=%async_computation.26 | async-start | bytes 1327104 | tf_op jit(solution)/shard_map/all_gather | solution.py:504
  674.2 191.5 %all-gather.26.cloned.1.call-start = ((), (), s32[]{:S(2)}) async-start(), calls=%async_computation.23 | async-start | bytes 1327104 | tf_op jit(solution)/shard_map/all_gather | solution.py:504
  696.8 184.5 %all-gather.32.cloned.1.call-start = ((), (), s32[]{:S(2)}) async-start(), calls=%async_computation.32 | async-start | bytes 1327104 | tf_op jit(solution)/shard_map/all_gather | solution.py:504
  719.2 188.2 %all-gather.30.cloned.1.call-start = ((), (), s32[]{:S(2)}) async-start(), calls=%async_computation.29 | async-start | bytes 1327104 | tf_op jit(solution)/shard_map/all_gather | solution.py:504
  730.1 52.8 %collective-permute-start.38 = (bf16[512,768]{0,1:T(8,128)(2,1)S(1)}, bf16[512,768]{0,1:T(8,128)(2,1)}, u32[]{:S(2)}, u32[]{:S(2)}) collective-permute-start(bf16[512,768]{0,1:T(8,128)(2,1)S(1)} %add_convert_fusion.8), channel_id=1, source_target_pairs={{0,1},{1,0},{2,3},{3,2},{4,5},{5,4},{6,7},{7,6},{8,9},{9,8},{10,11... | collective-permute-start | bytes 2359304 | tf_op jit(solution)/shard_map/ppermute | solution.py:320
  733.9 44.2 %collective-permute-start.14 = (bf16[512,192]{0,1:T(8,128)(2,1)}, bf16[512,192]{0,1:T(8,128)(2,1)S(1)}, u32[]{:S(2)}, u32[]{:S(2)}) collective-permute-start(bf16[512,192]{0,1:T(8,128)(2,1)} %get-tuple-element.195), channel_id=1, source_target_pairs={{0,3},{1,1},{2,7},{3,5},{4,2},{5,0},{6,6},{7,4},{8,11},{9,9},{10,1... | collective-permute-start | bytes 589832 | tf_op jit(solution)/shard_map/ppermute | solution.py:320
  738.0 41.6 %collective-permute-start.15 = (bf16[512,192]{0,1:T(8,128)(2,1)}, bf16[512,192]{0,1:T(8,128)(2,1)}, u32[]{:S(2)}, u32[]{:S(2)}) collective-permute-start(bf16[512,192]{0,1:T(8,128)(2,1)} %get-tuple-element.196), channel_id=1, source_target_pairs={{0,2},{1,0},{2,6},{3,4},{4,3},{5,1},{6,7},{7,5},{8,10},{9,8},{10,1... | collective-permute-start | bytes 589832 | tf_op jit(solution)/shard_map/ppermute | solution.py:320
  738.1 41.5 %collective-permute-start.16 = (bf16[512,192]{0,1:T(8,128)(2,1)}, bf16[512,192]{0,1:T(8,128)(2,1)}, u32[]{:S(2)}, u32[]{:S(2)}) collective-permute-start(bf16[512,192]{0,1:T(8,128)(2,1)} %get-tuple-element.197), channel_id=1, source_target_pairs={{0,1},{1,3},{2,5},{3,7},{4,0},{5,2},{6,4},{7,6},{8,9},{9,11},{10,1... | collective-permute-start | bytes 589832 | tf_op jit(solution)/shard_map/ppermute | solution.py:320
  740.1 39.5 %collective-permute-start.17 = (bf16[512,192]{0,1:T(8,128)(2,1)}, bf16[512,192]{0,1:T(8,128)(2,1)}, u32[]{:S(2)}, u32[]{:S(2)}) collective-permute-start(bf16[512,192]{0,1:T(8,128)(2,1)} %get-tuple-element.198), channel_id=1, source_target_pairs={{0,0},{1,2},{2,4},{3,6},{4,1},{5,3},{6,5},{7,7},{8,8},{9,10},{10,1... | collective-permute-start | bytes 589832 | tf_op jit(solution)/shard_map/ppermute | solution.py:320
  788.2 146.5 %all-gather.24.cloned.1.call-start = ((), (), s32[]{:S(2)}) async-start(), calls=%async_computation.20 | async-start | bytes 1658880 | tf_op jit(solution)/shard_map/all_gather | solution.py:504
  (163 other events, 2456.3 us)
Sparse Core Ops, SparseCore 0:
  11.8 57.7 all-gather.15
  71.4 37.1 all-gather.17
  110.4 37.4 all-gather.33
  149.9 59.7 all-gather.19
  211.4 36.3 all-gather.21
  259.7 37.0 all-gather.35
  412.3 35.4 reduce-scatter.24
  450.8 37.3 reduce-scatter.20
  491.3 37.3 reduce-scatter.32
  531.6 37.3 reduce-scatter.28
  572.1 42.3 reduce-scatter.16
  617.4 32.4 reduce-scatter.12
  652.2 22.0 reduce-scatter.26
  676.3 20.3 reduce-scatter.22
  698.9 20.2 reduce-scatter.34
  721.3 23.8 reduce-scatter.30
  747.4 33.5 reduce-scatter.18
  783.1 21.4 reduce-scatter.14
  806.7 22.3 all-gather.27
  831.0 24.0 all-gather.25
  857.1 24.0 all-gather.31
  883.3 24.0 all-gather.29
  909.4 25.2 all-gather.23

commit v2 on v1

v2 whole, which is shorter than its diff:
```python
import functools

import jax
import jax.numpy as jnp
from jax import lax
from jax.experimental import pallas as pl
from jax.experimental.pallas import tpu as pltpu
from jax.sharding import Mesh, PartitionSpec as P

HEADS = 12
EPS = 1e-06
ROWS_T = (((0,), (0,)), ((), ()))
COLS_T = (((1,), (1,)), ((), ()))
NEG = -1e30
AXES = ("g", "p", "c", "mp")
PIECES = 4
COST = 1.0
VMEM = 58 * 2**20
bf16 = jnp.bfloat16
f32 = jnp.float32


def dot_nt(a, b):
    return lax.dot_general(a, b, COLS_T, preferred_element_type=f32)


def dot_tn(a, b):
    return lax.dot_general(a, b, ROWS_T, preferred_element_type=f32)


def dot_nn(a, b):
    return jnp.dot(a, b, preferred_element_type=f32)


def cost(us):
    return pl.CostEstimate(flops=int(us * 1e9 * COST), bytes_accessed=int(us * 3e6 * COST), transcendentals=0)


def lane_mask(head, half):
    lanes = lax.broadcasted_iota(jnp.int32, (1, 2 * half), 1)
    return (lanes < half) if head == 0 else (lanes >= half)


def pick(mask, values):
    return jnp.where(mask, values, jnp.zeros_like(values))


def fwd_block(q, k, v, half, diagonal):
    out = None
    highs = []
    sums = []
    for head in (0, 1):
        mask = lane_mask(head, half)
        scores = dot_nt(q, pick(mask, k))
        if diagonal:
            rows = lax.broadcasted_iota(jnp.int32, scores.shape, 0)
            cols = lax.broadcasted_iota(jnp.int32, scores.shape, 1)
            scores = jnp.where(rows >= cols, scores, NEG)
        high = jnp.max(scores, axis=1, keepdims=True)
        chance = jnp.exp(scores - high)
        sums.append(jnp.sum(chance, axis=1, keepdims=True))
        highs.append(high)
        part = dot_nn(chance.astype(bf16), pick(mask, v))
        out = part if out is None else out + part
    first = lane_mask(0, half)
    shape = out.shape
    high = jnp.where(first, jnp.broadcast_to(highs[0], shape), jnp.broadcast_to(highs[1], shape))
    total = jnp.where(first, jnp.broadcast_to(sums[0], shape), jnp.broadcast_to(sums[1], shape))
    return out, high, total


def merge_into(acc_ref, high_ref, sum_ref, rows, part):
    out, high, total = part
    old = high_ref[rows, :]
    new = jnp.maximum(old, high)
    keep = jnp.exp(old - new)
    take = jnp.exp(high - new)
    acc_ref[rows, :] = acc_ref[rows, :] * keep + out * take
    sum_ref[rows, :] = sum_ref[rows, :] * keep + total * take
    high_ref[rows, :] = new


def fwd_local_kernel(quarter, half, s_ref, q_ref, k_ref, v_ref, acc_ref, high_ref, sum_ref):
    for i in (0, 1):
        rows = pl.ds(i * quarter, quarter)
        out, high, total = fwd_block(q_ref[rows, :], k_ref[rows, :], v_ref[rows, :], half, True)
        acc_ref[rows, :] = out
        high_ref[rows, :] = high
        sum_ref[rows, :] = total

    @pl.when(s_ref[0] > 0)
    def _():
        early = pl.ds(0, quarter)
        late = pl.ds(quarter, quarter)
        part = fwd_block(q_ref[late, :], k_ref[early, :], v_ref[early, :], half, False)
        merge_into(acc_ref, high_ref, sum_ref, late, part)


def fwd_remote_kernel(
    quarter, half, s_ref, q_ref, k_ref, v_ref, acc_in, high_in, sum_in, out_ref, lse_ref, acc_ref, high_ref, sum_ref
):
    acc_ref[...] = acc_in[...]
    high_ref[...] = high_in[...]
    sum_ref[...] = sum_in[...]

    @pl.when(s_ref[0] > 0)
    def _():
        early = pl.ds(0, quarter)
        late = pl.ds(quarter, quarter)
        part = fwd_block(q_ref[late, :], k_ref[early, :], v_ref[early, :], half, False)
        merge_into(acc_ref, high_ref, sum_ref, late, part)
        which = pl.ds(pl.multiple_of(s_ref[1] * quarter, quarter), quarter)
        part = fwd_block(q_ref[which, :], k_ref[which, :], v_ref[which, :], half, False)
        merge_into(acc_ref, high_ref, sum_ref, which, part)

    total = sum_ref[...]
    out_ref[...] = (acc_ref[...] / total).astype(out_ref.dtype)
    lse = high_ref[...] + jnp.log(total)
    flat = lse.T
    lse_ref[0, 0:1, :] = flat[0:1, :]
    lse_ref[0, 1:2, :] = flat[half : half + 1, :]


def bwd_block(q, do, k, v, lse, inner, half, diagonal):
    k_t = k.T
    d_key = d_value = d_query_t = None
    subl = lax.broadcasted_iota(jnp.int32, (2 * half, 1), 0)
    for head in (0, 1):
        mask = lane_mask(head, half)
        scores = dot_nt(pick(mask, k), q)
        chance = jnp.exp(scores - lse[head : head + 1, :])
        if diagonal:
            keys = lax.broadcasted_iota(jnp.int32, scores.shape, 0)
            queries = lax.broadcasted_iota(jnp.int32, scores.shape, 1)
            chance = jnp.where(queries >= keys, chance, 0.0)
        d_chance = dot_nt(pick(mask, v), do)
        d_scores = (chance * (d_chance - inner[head : head + 1, :])).astype(bf16)
        part_v = dot_nn(chance.astype(bf16), pick(mask, do))
        part_k = dot_nn(d_scores, pick(mask, q))
        row_mask = (subl < half) if head == 0 else (subl >= half)
        part_q = dot_nn(pick(row_mask, k_t), d_scores)
        d_value = part_v if d_value is None else d_value + part_v
        d_key = part_k if d_key is None else d_key + part_k
        d_query_t = part_q if d_query_t is None else d_query_t + part_q
    return d_query_t, d_key, d_value


def bwd_remote_kernel(
    quarter, half, s_ref, q_ref, k_ref, v_ref, o_ref, do_ref, lse_ref,
    dqt_ref, dk_ref, dv_ref, inner_ref, sums_ref, ak_ref, av_ref
):
    flat = (o_ref[...].astype(f32) * do_ref[...].astype(f32)).T
    inner_ref[0, 0:1, :] = jnp.sum(flat[:half, :], axis=0, keepdims=True)
    inner_ref[0, 1:2, :] = jnp.sum(flat[half:, :], axis=0, keepdims=True)
    dqt_ref[...] = jnp.zeros_like(dqt_ref)
    ak_ref[...] = jnp.zeros_like(ak_ref)
    av_ref[...] = jnp.zeros_like(av_ref)

    @pl.when(s_ref[0] > 0)
    def _():
        def job(q_rows, k_rows):
            dqt, dk, dv = bwd_block(
                q_ref[q_rows, :],
                do_ref[q_rows, :],
                k_ref[k_rows, :],
                v_ref[k_rows, :],
                lse_ref[0, 0:2, q_rows],
                inner_ref[0, 0:2, q_rows],
                half,
                False,
            )
            dqt_ref[0, :, q_rows] += dqt
            ak_ref[k_rows, :] += dk
            av_ref[k_rows, :] += dv

        job(pl.ds(quarter, quarter), pl.ds(0, quarter))
        which = pl.ds(pl.multiple_of(s_ref[1] * quarter, quarter), quarter)
        job(which, which)

    dk_ref[...] = ak_ref[...].astype(dk_ref.dtype)
    dv_ref[...] = av_ref[...].astype(dv_ref.dtype)
    sums_ref[0, 0:1, :] = jnp.sum(av_ref[...], axis=0, keepdims=True)


def bwd_local_kernel(
    quarter, half, scale, s_ref, q_ref, k_ref, v_ref, do_ref, lse_ref, inner_ref, dqt_in,
    dq_ref, dk_ref, dv_ref, sums_ref, dqt_ref, ak_ref, av_ref
):
    for i in (0, 1):
        rows = pl.ds(i * quarter, quarter)
        dqt, dk, dv = bwd_block(
            q_ref[rows, :], do_ref[rows, :], k_ref[rows, :], v_ref[rows, :],
            lse_ref[0, 0:2, rows], inner_ref[0, 0:2, rows], half, True,
        )
        dqt_ref[:, rows] = dqt_in[0, :, rows] + dqt
        ak_ref[rows, :] = dk
        av_ref[rows, :] = dv

    @pl.when(s_ref[0] > 0)
    def _():
        early = pl.ds(0, quarter)
        late = pl.ds(quarter, quarter)
        dqt, dk, dv = bwd_block(
            q_ref[late, :], do_ref[late, :], k_ref[early, :], v_ref[early, :],
            lse_ref[0, 0:2, late], inner_ref[0, 0:2, late], half, False,
        )
        dqt_ref[:, late] += dqt
        ak_ref[early, :] += dk
        av_ref[early, :] += dv

    dq = dqt_ref[...].T * scale
    dq_ref[...] = dq.astype(dq_ref.dtype)
    dk_ref[...] = ak_ref[...].astype(dk_ref.dtype)
    dv_ref[...] = av_ref[...].astype(dv_ref.dtype)
    sums_ref[0, 0:1, :] = jnp.sum(dq, axis=0, keepdims=True)
    sums_ref[0, 1:2, :] = jnp.sum(av_ref[...], axis=0, keepdims=True)


class Attention:
    def __init__(self, tokens, heads, size):
        self.tokens, self.pairs, self.size = tokens, heads // 2, size
        self.quarter = tokens // 2
        self.width = 2 * size

    def rows(self, first):
        return pl.BlockSpec((self.tokens, self.width), lambda j, s: (0, first + j))

    def flat(self):
        return pl.BlockSpec((1, 8, self.tokens), lambda j, s: (j, 0, 0))

    def small(self):
        return pl.BlockSpec((1, 8, self.width), lambda j, s: (j, 0, 0))

    def turned(self):
        return pl.BlockSpec((1, self.width, self.tokens), lambda j, s: (j, 0, 0))

    def call(self, kernel, in_specs, out_specs, out_shape, scratch, blocks, dots):
        return pl.pallas_call(
            kernel,
            out_shape=out_shape,
            grid_spec=pltpu.PrefetchScalarGridSpec(
                num_scalar_prefetch=1,
                grid=(self.pairs,),
                in_specs=in_specs,
                out_specs=out_specs,
                scratch_shapes=scratch,
            ),
            compiler_params=pltpu.CompilerParams(vmem_limit_bytes=VMEM),
            cost_estimate=cost(blocks * dots * 1.2 + 2),
        )

    def shape(self, dtype):
        return jax.ShapeDtypeStruct((self.tokens, self.pairs * self.width), dtype)

    def flat_shape(self):
        return jax.ShapeDtypeStruct((self.pairs, 8, self.tokens), f32)

    def scratch(self):
        return pltpu.VMEM((self.tokens, self.width), f32)

    def forward_local(self, flags, qkv):
        n = self.pairs
        return self.call(
            functools.partial(fwd_local_kernel, self.quarter, self.size),
            [self.rows(0), self.rows(n), self.rows(2 * n)],
            [self.rows(0)] * 3,
            [self.shape(f32)] * 3,
            [],
            3,
            2,
        )(flags, qkv, qkv, qkv)

    def forward_remote(self, flags, qkv, kv, acc, high, total):
        n = self.pairs
        return self.call(
            functools.partial(fwd_remote_kernel, self.quarter, self.size),
            [self.rows(0), self.rows(0), self.rows(n), self.rows(0), self.rows(0), self.rows(0)],
            [self.rows(0), self.flat()],
            [self.shape(bf16), self.flat_shape()],
            [self.scratch()] * 3,
            2,
            2,
        )(flags, qkv, kv, kv, acc, high, total)

    def backward_remote(self, flags, qkv, kv, out, d_out, lse):
        n = self.pairs
        return self.call(
            functools.partial(bwd_remote_kernel, self.quarter, self.size),
            [self.rows(0), self.rows(0), self.rows(n), self.rows(0), self.rows(0), self.flat()],
            [self.turned(), self.rows(0), self.rows(0), self.flat(), self.small()],
            [
                jax.ShapeDtypeStruct((n, self.width, self.tokens), f32),
                self.shape(bf16),
                self.shape(bf16),
                self.flat_shape(),
                jax.ShapeDtypeStruct((n, 8, self.width), f32),
            ],
            [self.scratch()] * 2,
            2,
            5,
        )(flags, qkv, kv, kv, out, d_out, lse)

    def backward_local(self, flags, qkv, d_out, lse, inner, dqt):
        n = self.pairs
        return self.call(
            functools.partial(bwd_local_kernel, self.quarter, self.size, float(self.size) ** -0.5),
            [self.rows(0), self.rows(n), self.rows(2 * n), self.rows(0), self.flat(), self.flat(), self.turned()],
            [self.rows(0)] * 3 + [self.small()],
            [self.shape(bf16)] * 3 + [jax.ShapeDtypeStruct((n, 8, self.width), f32)],
            [pltpu.VMEM((self.width, self.tokens), f32), self.scratch(), self.scratch()],
            3,
            5,
        )(flags, qkv, qkv, qkv, d_out, lse, inner, dqt)


def norm_of(x):
    total = jnp.sum(x, axis=1, keepdims=True)
    squares = jnp.sum(x * x, axis=1, keepdims=True)
    return total, lax.rsqrt((squares + total * total) / x.shape[1] + EPS)


def norm_back(x, d_normed):
    total, factor = norm_of(x)
    inner = jnp.sum(d_normed * x, axis=1, keepdims=True)
    term = factor * factor * factor * inner / x.shape[1]
    return factor * d_normed - term * (x + total)


def chunks(rows, step=128):
    return [pl.ds(i, step) for i in range(0, rows, step)]


def keep_of(width):
    return jnp.where(lax.broadcasted_iota(jnp.int32, (1, width), 1) < width - 1, 1.0, 0.0)


def vmem(count=1):
    return [pl.BlockSpec(memory_space=pltpu.VMEM)] * count


def smem():
    return [pl.BlockSpec(memory_space=pltpu.SMEM)]


def hbm(count=1):
    return [pl.BlockSpec(memory_space=pltpu.HBM)] * count


def shaped(shape, dtype):
    return jax.ShapeDtypeStruct(shape, dtype)


def kernel_call(kernel, us, mib, in_specs, out_specs, out_shape, scratch=(), aliases=None):
    return pl.pallas_call(
        kernel,
        input_output_aliases=aliases or {},
        in_specs=in_specs,
        out_specs=out_specs,
        out_shape=out_shape,
        scratch_shapes=list(scratch),
        compiler_params=pltpu.CompilerParams(vmem_limit_bytes=VMEM),
        cost_estimate=cost(us),
    )


def run(copies, what):
    for copy in copies:
        getattr(copy, what)()


def quarter_kernel(normed, s_ref, *refs):
    blocks, x_ref = refs[:4], refs[4]
    quarter, width = x_ref.shape
    for spot in range(4):

        @pl.when(s_ref[0] == spot)
        def _(spot=spot):
            for rows in chunks(quarter):
                whole = jnp.concatenate([blocks[j ^ spot][rows, :].astype(f32) for j in range(4)], axis=1)
                if normed:
                    whole = whole * keep_of(width)
                    _, factor = norm_of(whole)
                    refs[5][rows, :] = (whole * factor).astype(bf16)
                x_ref[rows, :] = whole.astype(bf16)


def quarter_rows(blocks, spot, normed):
    quarter, part = blocks[0].shape
    shapes = [shaped((quarter, 4 * part), bf16)] * (2 if normed else 1)
    return kernel_call(
        functools.partial(quarter_kernel, normed), 2, 16, smem() + vmem(4), vmem(len(shapes)), shapes
    )(spot[None], *blocks)


def both_kernel(s_ref, mine_ref, other_ref, x_ref, n_ref):
    quarter = mine_ref.shape[0]
    for ref, core in ((mine_ref, s_ref[0]), (other_ref, 1 - s_ref[0])):
        for start in range(0, quarter, 128):
            x = ref[pl.ds(start, 128), :].astype(f32)
            rows = pl.ds(pl.multiple_of(core * quarter + start, 128), 128)
            x_ref[rows, :] = x
            _, factor = norm_of(x)
            n_ref[rows, :] = (x * factor).astype(bf16)


def both_rows(mine, other, core):
    shape = (2 * mine.shape[0], mine.shape[1])
    return kernel_call(both_kernel, 2, 16, smem() + vmem(2), vmem(2), [shaped(shape, f32), shaped(shape, bf16)])(
        core[None], mine, other
    )


class Stage:
    def __init__(self, ins, in_sems, outs, out_sems):
        self.ins = [self.parts(a, b, sem) for (a, b), sem in zip(ins, in_sems)]
        self.outs = [(b, a, sem) for (a, b), sem in zip(outs, out_sems)]
        self.targets = [a for a, _ in outs]
        self.waited = set()
        self.pushed = []
        for copies in self.ins:
            run(copies, "start")

    @staticmethod
    def parts(source, target, sem):
        count = sem.shape[0]
        rows = source.shape[0] // count
        if count == 1:
            return [pltpu.make_async_copy(source, target, sem.at[0])]
        cut = [pl.ds(i * rows, rows) for i in range(count)]
        return [pltpu.make_async_copy(source.at[r], target.at[r], sem.at[i]) for i, r in enumerate(cut)]

    def need(self, *which, part=None):
        for i in which:
            for k, copy in enumerate(self.ins[i]):
                if (part is None or k == part % len(self.ins[i])) and (i, k) not in self.waited:
                    self.waited.add((i, k))
                    copy.wait()

    def push(self, *which, part=0):
        for i in which:
            source, target, sem = self.outs[i]
            rows = source.shape[0] // sem.shape[0]
            cut = pl.ds(part * rows, rows)
            copy = pltpu.make_async_copy(source.at[cut], target.at[cut], sem.at[part])
            copy.start()
            self.pushed.append(copy)

    def done(self):
        run(self.pushed, "wait")


def staged(body, us, scalars, ins, raw, outs, raw_outs=(), small=(), scratch=(), single=False, aliases=None):
    n = [len(scalars), len(ins), len(raw), len(outs), len(raw_outs), len(small), len(ins), len(outs), len(scratch)]
    n += [len(ins), len(outs)]

    def kernel(*refs):
        groups = []
        at = 0
        for count in n:
            groups.append(refs[at : at + count])
            at += count
        sc, hi, hr, ho, hro, sm, vi, vo, ex, si, so = groups
        stage = Stage(list(zip(hi, vi)), si, list(zip(ho, vo)), so)
        body(stage, sc, vi, hr, vo, hro, sm, ex)
        stage.done()

    held = [pltpu.VMEM(a.shape, a.dtype) for a, _ in ins] + [pltpu.VMEM(shape, dtype) for shape, dtype, _ in outs]
    size = sum(a.size * a.dtype.itemsize for a, _ in ins)
    for shape, dtype, _ in outs:
        count = jnp.dtype(dtype).itemsize
        for extent in shape:
            count *= extent
        size += count
    for one in scratch:
        if jnp.issubdtype(one.dtype, jnp.floating):
            count = jnp.dtype(one.dtype).itemsize
            for extent in one.shape:
                count *= extent
            size += count
    got = kernel_call(
        kernel,
        us,
        size // 2**20 + 12,
        smem() * len(scalars) + hbm(len(ins) + len(raw)),
        hbm(len(outs) + len(raw_outs)) + vmem(len(small)),
        [shaped(shape, dtype) for shape, dtype, _ in outs] + list(raw_outs) + list(small),
        held + list(scratch) + [sems(k) for _, k in ins] + [sems(k) for _, _, k in outs],
        aliases or {},
    )(*scalars, *[a for a, _ in ins], *raw)
    return got[0] if single else got


def sems(count):
    return pltpu.SemaphoreType.DMA((count,))


def next_rows(stage, x, a, b, bias, x_out, n_out):
    keep = keep_of(x.shape[1])
    rows = x.shape[0] // 4
    stage.need(3)
    for part in range(4):
        stage.need(0, 1, 2, part=part)
        for start in range(part * rows, part * rows + rows, 128):
            at = pl.ds(start, 128)
            value = x[at, :] + (a[at, :].astype(f32) + b[at, :].astype(f32) + bias[...]) * keep
            x_out[at, :] = value
            _, factor = norm_of(value)
            n_out[at, :] = (value * factor).astype(bf16)
        stage.push(0, 1, part=part)


def next_stream(x, a, b, bias):
    def body(stage, scalars, ins, raw, outs, raw_outs, small, scratch):
        next_rows(stage, *ins, *outs)

    return staged(
        body, 3, [], [(x, 4), (a, 4), (b, 4), (bias[None], 1)], [], [(x.shape, f32, 4), (x.shape, bf16, 4)]
    )


def gelu_parts(x):
    a = 0.7978845608028654
    square = x * x
    s = 0.5 + 0.5 * jnp.tanh(x * (a + (a * 0.044715) * square))
    value = x * s
    slope = s + (value - value * s) * (2 * a + (6 * a * 0.044715) * square)
    return value.astype(bf16), slope.astype(bf16)


class Units:
    def __init__(self, buffers, blocks, turned):
        self.buffers, self.blocks, self.turned = buffers, blocks, turned

    def spot(self, where, step, column):
        if not self.turned:
            return step, column
        return jnp.bitwise_xor(where[2], step), jnp.bitwise_xor(where[0], column)

    def copies(self, refs, where, first, target, sem):
        count = target.shape[2]
        copies = [[], [], [], []]
        for i, (step, column, buffer, index) in enumerate(self.blocks):
            source = refs[buffer].at[index + (pl.ds(first, count),)]
            chip, spot = self.spot(where, step, column)
            copies[step].append(pltpu.make_async_copy(source, target.at[chip, spot], sem.at[i]))
        return copies


def turned_units(pieces):
    blocks = []
    for buffer, (array, column, chip) in enumerate(pieces):
        blocks += [(chip + i, column, buffer, (i,)) for i in range(array.shape[0])]
    return Units([place[0] for place in pieces], blocks, True)


def plain_units(array):
    return Units([array], [(chip, column, 0, (column, chip)) for chip in range(4) for column in range(4)], False)


def column_of(row):
    return jnp.broadcast_to(row, (8, row.shape[1])).T[:, 0:1]


def row_of(column):
    return jnp.broadcast_to(column, (column.shape[0], 128)).T[0:1, :]


def mlp_forward(where, x, a, b, bias, units, step, b_up):
    tokens, width = x.shape
    part = 4 * step

    def body(stage, scalars, ins, raw, outs, raw_outs, small, scratch):
        up, down, up_sem, down_sem = scratch
        x1, n1, g, slope, out = outs
        up_copies = units.copies(raw, scalars[0], 0, up, up_sem)
        down_copies = units.copies(raw, scalars[0], step, down, down_sem)
        for copies in up_copies + down_copies:
            run(copies, "start")
        next_rows(stage, *ins[:4], x1, n1)
        stage.need(4)
        for copies in up_copies:
            run(copies, "wait")
        for t in range(4):
            chip, _ = units.spot(scalars[0], t, 0)
            rows = pl.ds(pl.multiple_of(chip * part, part), part)
            h = dot_nt(up[chip].reshape(part, width), n1[...]) + column_of(ins[4][:, rows])
            g[rows, :], slope[rows, :] = gelu_parts(h)
        stage.push(2, 3)
        for copies in down_copies:
            run(copies, "wait")
        for i, first in enumerate(range(0, width, 256)):
            columns = pl.ds(first, 256)
            out[:, columns] = dot_tn(g[...], down[:, :, :, columns].reshape(4 * part, 256)).astype(bf16)
        stage.push(4)

    hidden = 4 * part
    return staged(
        body,
        14,
        [where],
        [(x, 4), (a, 4), (b, 4), (bias[None], 1), (b_up[None], 1)],
        units.buffers,
        [
            (x.shape, f32, 4),
            (x.shape, bf16, 4),
            ((hidden, tokens), bf16, 1),
            ((hidden, tokens), bf16, 1),
            (x.shape, bf16, 1),
        ],
        scratch=[pltpu.VMEM((4, 4, step, width), bf16)] * 2 + [sems(16)] * 2,
    )


def mlp_backward(where, before, n1, g, slope, units, step):
    first = len(before) == 2
    tokens, width = n1.shape
    part = 4 * step
    hidden = 4 * part

    def body(stage, scalars, ins, raw, outs, raw_outs, small, scratch):
        up, down, dm, dh, gw, up_sem, down_sem, gw_sem = scratch
        dx_out, dn_out = outs
        place = scalars[0]
        count = len(before)
        n1_in, s_in, g_in = ins[count:]
        down_copies = units.copies(raw, place, step, down, down_sem)
        up_copies = units.copies(raw, place, 0, up, up_sem)
        for copies in down_copies + up_copies:
            run(copies, "start")
        keep = keep_of(width)
        total = jnp.zeros((1, width), f32)
        rows = tokens // 4
        for k in range(4):
            for start in range(k * rows, k * rows + rows, 128):
                if first:
                    stage.need(k // 2, part=k)
                    at = (k % 2) * rows + start - k * rows
                    core = place[1] if k < 2 else 1 - place[1]
                    dx = ins[k // 2][pl.ds(at, 128), :].astype(f32)
                    spot = pl.ds(pl.multiple_of(core * (tokens // 2) + at, 128), 128)
                else:
                    stage.need(0, 1, 2, 3, part=k)
                    spot = pl.ds(start, 128)
                    dn = ins[2][spot, :].astype(f32) + ins[3][spot, :].astype(f32)
                    dx = ins[0][spot, :] + norm_back(ins[1][spot, :], dn)
                dx_out[spot, :] = dx
                low = (dx * keep).astype(bf16)
                dm[spot, :] = low
                total = total + jnp.sum(low.astype(f32), axis=0, keepdims=True)
        stage.push(0)
        bu_ref, bd_ref = small
        bd_ref[...] = jnp.broadcast_to(total, bd_ref.shape)
        stage.need(count, count + 1, count + 2)
        for copies in down_copies:
            run(copies, "wait")
        stores = []
        for t in range(4):
            chip, _ = units.spot(place, t, 0)
            at = pl.ds(pl.multiple_of(chip * part, part), part)
            d_hidden = dot_nt(down[chip].reshape(part, width), dm[...]) * s_in[at, :].astype(f32)
            bu_ref[:, at] = jnp.broadcast_to(row_of(jnp.sum(d_hidden, axis=1, keepdims=True)), (8, part))
            d_hidden = d_hidden.astype(bf16)
            dh[at, :] = d_hidden
            gw[t, :, 0:step, :] = dot_nn(d_hidden, n1_in[...]).astype(bf16).reshape(4, step, width)
            gw[t, :, step:, :] = dot_nn(g_in[at, :], dm[...]).astype(bf16).reshape(4, step, width)
            for j in range(4):
                if units.turned:
                    near, far, kept = raw_outs
                    target = {
                        (2, 0): near.at[0], (3, 0): near.at[1], (1, 1): far.at[0], (3, 1): far.at[1],
                        (0, 0): kept.at[0], (1, 0): kept.at[1], (0, 1): kept.at[2], (2, 1): kept.at[3],
                    }[(j, t // 2)].at[t % 2]
                    source = gw.at[t, jnp.bitwise_xor(place[0], j)]
                else:
                    target = raw_outs[0].at[j, t]
                    source = gw.at[t, j]
                stores.append(pltpu.make_async_copy(source, target, gw_sem.at[4 * t + j]))
        run(stores, "start")
        stage.pushed.extend(stores)
        for copies in up_copies:
            run(copies, "wait")
        for first_column in range(0, width, 256):
            columns = pl.ds(first_column, 256)
            dn_out[:, columns] = dot_tn(dh[...], up[:, :, :, columns].reshape(hidden, 256)).astype(bf16)
        stage.push(1)

    ins = [(a, 2) for a in before] if first else [(a, 4) for a in before]
    if units.turned:
        raw_outs = [shaped((2, 2, 2 * step, width), bf16)] * 2 + [shaped((4, 2, 2 * step, width), bf16)]
    else:
        raw_outs = [shaped((4, 4, 2 * step, width), bf16)]
    return staged(
        body,
        18,
        [where],
        ins + [(n1, 1), (slope, 1), (g, 1)],
        units.buffers,
        [((tokens, width), f32, 1), ((tokens, width), bf16, 1)],
        raw_outs,
        [shaped((8, hidden), f32), shaped((8, width), f32)],
        [pltpu.VMEM((4, 4, step, width), bf16)] * 2
        + [pltpu.VMEM((tokens, width), bf16), pltpu.VMEM((hidden, tokens), bf16)]
        + [pltpu.VMEM((4, 4, 2 * step, width), bf16)]
        + [sems(16)] * 3,
    )


def out_backward(dx, x, a, b, rows):
    tokens, width = dx.shape
    heads = rows.shape[0]

    def body(stage, scalars, ins, raw, outs, raw_outs, small, scratch):
        w_ref, w_sem = scratch
        load = pltpu.make_async_copy(raw[0], w_ref, w_sem.at[0])
        load.start()
        dx1, da_out, do = outs
        keep = keep_of(width)
        total = jnp.zeros((1, width), f32)
        load.wait()
        for k in range(4):
            stage.need(0, 1, 2, 3, part=k)
            for start in (0, 128):
                at = pl.ds(k * 256 + start, 128)
                dn = ins[2][at, :].astype(f32) + ins[3][at, :].astype(f32)
                value = ins[0][at, :] + norm_back(ins[1][at, :], dn)
                dx1[at, :] = value
                da = (value * keep).astype(bf16)
                da_out[at, :] = da
                total = total + jnp.sum(da.astype(f32), axis=0, keepdims=True)
            at = pl.ds(k * 256, 256)
            do[at, :] = dot_nt(da_out[at, :], w_ref[...]).astype(bf16)
            stage.push(0, 1, 2, part=k)
        small[0][...] = jnp.broadcast_to(total, small[0].shape)

    return staged(
        body,
        5,
        [],
        [(dx, 4), (x, 4), (a, 4), (b, 4)],
        [rows],
        [((tokens, width), f32, 4), ((tokens, width), bf16, 4), ((tokens, heads), bf16, 4)],
        small=[shaped((8, width), f32)],
        scratch=[pltpu.VMEM((heads, width), bf16), sems(1)],
    )


def piece_copies(where, pieces, rows, held, sem):
    copies = []
    for i in range(4):
        for j in (0, 1):
            if len(pieces) > 1:
                spot = 2 * jnp.bitwise_xor(where[0], i) + jnp.bitwise_xor(where[1], j)
                source = pieces[4 * j + i]
            else:
                spot = 2 * i + j
                source = pieces[0].at[spot]
            copies.append(
                pltpu.make_async_copy(source.at[pl.ds(0, rows)], held.at[spot], sem.at[2 * i + j])
            )
    return copies


def units_out(where, layer, layers, pieces, step, before):
    width = pieces[0].shape[-1]
    hidden = 8 * step
    count = len(pieces)

    def body(stage, scalars, ins, raw, outs, raw_outs, small, scratch):
        held, up, down, in_sem, out_sem = scratch
        copies = piece_copies(scalars[0], raw[:count], 2 * step, held, in_sem)
        run(copies, "start")
        run(copies, "wait")
        for i in range(8):
            down[pl.ds(i * step, step), :] = held[i, step:, :].astype(f32)
        store = pltpu.make_async_copy(down, raw_outs[1].at[layer], out_sem.at[0])
        store.start()
        up[...] = held[:, :step, :].reshape(hidden, width).astype(f32).T
        last = pltpu.make_async_copy(up, raw_outs[0].at[layer], out_sem.at[1])
        last.start()
        run([store, last], "wait")

    return staged(
        body,
        5,
        [where],
        [],
        list(pieces) + list(before),
        [],
        [shaped((layers, width, hidden), f32), shaped((layers, hidden, width), f32)],
        (),
        [
            pltpu.VMEM((8, 2 * step, width), bf16),
            pltpu.VMEM((width, hidden), f32),
            pltpu.VMEM((hidden, width), f32),
            sems(8),
            sems(2),
        ],
        aliases={1 + count: 0, 2 + count: 1} if before else {},
    )


def heads_out(where, layer, layers, pieces, part, before):
    rows, width = pieces[0].shape[-2:]
    local = 8 * part
    count = len(pieces)

    def body(stage, scalars, ins, raw, outs, raw_outs, small, scratch):
        held, value, in_sem, out_sem = scratch
        copies = piece_copies(scalars[0], raw[:count], rows, held, in_sem)
        run(copies, "start")
        run(copies, "wait")
        stores = []
        for kind in range(4):
            value[kind] = held[:, kind * part : (kind + 1) * part, :].astype(f32).reshape(local, width)
            target = raw_outs[0].at[layer, kind] if kind < 3 else raw_outs[1].at[layer]
            stores.append(pltpu.make_async_copy(value.at[kind], target, out_sem.at[kind]))
            stores[-1].start()
        small[0][...] = jnp.sum(held[:, rows - 8 :, :].astype(f32), axis=0)
        run(stores, "wait")

    return staged(
        body,
        3,
        [where],
        [],
        list(pieces) + list(before),
        [],
        [shaped((layers, 3, local, width), f32), shaped((layers, local, width), f32)],
        [shaped((8, width), f32)],
        [pltpu.VMEM((8, rows, width), bf16), pltpu.VMEM((4, local, width), f32), sems(8), sems(4)],
        aliases={1 + count: 0, 2 + count: 1} if before else {},
    )


def heads_copies(kinds, part, s_ref, refs, turned, outs, sem):
    copies = []
    for kind in range(kinds):
        if turned:
            rows = pl.ds(kind * part, part)
            sources = [(refs[j].at[pl.ds(2 * h, 2), rows], j, h) for j in range(3) for h in (0, 1)]
            sources += [(refs[3].at[:, rows], 3, 0), (refs[4].at[:, rows], 3, 1)]
        else:
            first = refs[0].shape[2] - kinds * part
            pair = pl.ds(2 * s_ref[1], 2)
            sources = [(refs[0].at[j, pair, pl.ds(first + kind * part, part)], j, 0) for j in range(4)]
            sources += [(refs[1].at[j, :, pl.ds(kind * part, part)], j, 1) for j in range(4)]
        out = outs[0].at[kind] if kind < kinds - 1 else outs[1].at[0]
        for i, (source, j, h) in enumerate(sources):
            column = jnp.bitwise_xor(s_ref[0], j) if turned else j
            spot = 2 * column + jnp.bitwise_xor(s_ref[1], h)
            copies.append(pltpu.make_async_copy(source, out.at[pl.ds(0, 2), spot], sem.at[kind * 8 + i]))
    return copies


def heads_rows(refs, where, kinds, part, turned):
    width = refs[0].shape[-1]

    def body(stage, scalars, ins, raw, outs, raw_outs, small, scratch):
        copies = heads_copies(kinds, part, scalars[0], raw, turned, outs, scratch[0])
        run(copies, "start")
        for kind in range(kinds):
            run(copies[8 * kind : 8 * kind + 8], "wait")
            if kind < kinds - 1:
                stage.push(0, part=kind)
            else:
                stage.push(1)

    got = staged(
        body,
        3,
        [where],
        [],
        refs,
        [((kinds - 1, 2, 8, part, width), bf16, kinds - 1), ((1, 2, 8, part, width), bf16, 1)],
        scratch=[sems(8 * kinds)],
    )
    return [value.reshape(-1, width) for value in got]


def heads_terms(where, dq, dk, dv, o, dkr, dvr, n, far_mine, far_other, da, part, turned):
    tokens, width = n.shape
    quarter = tokens // 2

    def body(stage, scalars, ins, raw, outs, raw_outs, small, scratch):
        value_ref, sem = scratch
        s_ref = scalars[0]
        mine = pl.ds(pl.multiple_of(s_ref[1] * quarter, quarter), quarter)
        other = pl.ds(pl.multiple_of((1 - s_ref[1]) * quarter, quarter), quarter)

        def near(i, y):
            stage.need(i, y)
            return dot_tn(ins[i][...], ins[y][...])

        def far(i):
            stage.need(i, 7, 8)
            return dot_tn(ins[i][mine, :], ins[7][...]) + dot_tn(ins[i][other, :], ins[8][...])

        terms = (lambda: near(0, 6), lambda: near(1, 6) + far(4), lambda: near(2, 6) + far(5), lambda: near(3, 9))
        for kind, term in enumerate(terms):
            value_ref[kind] = term().astype(bf16).reshape(2, 8, part, width)
            rows = pl.ds(kind * part, part)
            for j in range(4):
                for mine_too in (0, 1):
                    if turned:
                        target = raw_outs[j].at[pl.ds(2 * (1 - mine_too), 2), rows]
                        column = jnp.bitwise_xor(s_ref[0], j)
                    else:
                        target, column = raw_outs[1 - mine_too].at[j, :, rows], j
                    spot = 2 * column + (s_ref[1] if mine_too else 1 - s_ref[1])
                    copy = pltpu.make_async_copy(
                        value_ref.at[kind, :, spot], target, sem.at[kind * 8 + 2 * j + mine_too]
                    )
                    copy.start()
                    stage.pushed.append(copy)

    ins = [dq, dk, dv, o, dkr, dvr, n, far_mine, far_other, da]
    if turned:
        raw_outs = [shaped((4, 4 * part, width), bf16)] * 4
    else:
        raw_outs = [shaped((4, 2, 4 * part, width), bf16)] * 2
    return staged(
        body,
        6,
        [where],
        [(a, 1) for a in ins],
        [],
        [],
        raw_outs,
        scratch=[pltpu.VMEM((4, 2, 8, part, width), bf16), sems(32)],
    )


def far_project(where, mine, other, rows, offset):
    quarter, width = mine.shape
    heads = rows.shape[0] // 3

    def body(stage, scalars, ins, raw, outs, raw_outs, small, scratch):
        w_ref, w_sem = scratch
        load = pltpu.make_async_copy(raw[0].at[pl.ds(heads, 2 * heads)], w_ref, w_sem.at[0])
        load.start()
        stage.need(2)
        load.wait()
        for i in (0, 1):
            stage.need(i)
            core = scalars[0][1] if i == 0 else 1 - scalars[0][1]
            at = pl.ds(pl.multiple_of(core * quarter, quarter), quarter)
            outs[0][at, :] = (dot_nt(ins[i][...], w_ref[...]) + ins[2][...]).astype(bf16)
        stage.push(0)

    return staged(
        body,
        2,
        [where],
        [(mine, 1), (other, 1), (offset[None], 1)],
        [rows],
        [((2 * quarter, 2 * heads), bf16, 1)],
        scratch=[pltpu.VMEM((2 * heads, width), bf16), sems(1)],
        single=True,
    )


def far_terms(where, dkr, dvr, rows):
    quarter, width = dkr.shape[0] // 2, rows.shape[1]
    heads = dkr.shape[1]

    def body(stage, scalars, ins, raw, outs, raw_outs, small, scratch):
        w_ref, w_sem = scratch
        load = pltpu.make_async_copy(raw[0].at[pl.ds(heads, 2 * heads)], w_ref, w_sem.at[0])
        load.start()
        stage.need(0, 1)
        load.wait()
        for i, core in enumerate((1 - scalars[0][1], scalars[0][1])):
            at = pl.ds(pl.multiple_of(core * quarter, quarter), quarter)
            value = dot_nn(ins[0][at, :], w_ref[pl.ds(0, heads), :])
            outs[i][...] = (value + dot_nn(ins[1][at, :], w_ref[pl.ds(heads, heads), :])).astype(bf16)
            stage.push(i)

    return staged(
        body,
        2,
        [where],
        [(dkr, 1), (dvr, 1)],
        [rows],
        [((quarter, width), bf16, 1)] * 2,
        scratch=[pltpu.VMEM((2 * heads, width), bf16), sems(1)],
    )


def near_terms(where, dq, dk, dv, back, rows):
    tokens, heads = dq.shape
    width = rows.shape[1]
    quarter = tokens // 2

    def body(stage, scalars, ins, raw, outs, raw_outs, small, scratch):
        w_ref, w_sem = scratch
        load = pltpu.make_async_copy(raw[0].at[pl.ds(0, 3 * heads)], w_ref, w_sem.at[0])
        load.start()
        stage.need(0, 1, 2, 3)
        load.wait()
        for core in (0, 1):
            at = pl.ds(core * quarter, quarter)
            value = ins[3][...].astype(f32) * jnp.where(scalars[0][1] == core, 1.0, 0.0)
            for i in range(3):
                value = value + dot_nn(ins[i][at, :], w_ref[pl.ds(i * heads, heads), :])
            outs[0][at, :] = value.astype(bf16)
            stage.push(0, part=core)

    return staged(
        body,
        3,
        [where],
        [(dq, 1), (dk, 1), (dv, 1), (back, 1)],
        [rows],
        [((tokens, width), bf16, 2)],
        scratch=[pltpu.VMEM((3 * heads, width), bf16), sems(1)],
        single=True,
    )


def hold(value, *marks):
    return value if not marks else lax.optimization_barrier((value,) + marks)[0]


class Moves:
    def __init__(self, groups, pieces, chips):
        self.sizes = (groups, pieces, 2, chips)
        self.p = lax.axis_index("p")
        self.c = lax.axis_index("c")
        self.z = lax.axis_index("mp")
        self.spot = 2 * (self.z % 2) + self.c

    def permute(self, value, target):
        groups, pieces, cores, chips = self.sizes
        place = lambda g, p, c, z: ((g * pieces + p) * cores + c) * chips + z
        pairs = [
            (place(g, p, c, z), place(*target(g, p, c, z)))
            for g in range(groups)
            for p in range(pieces)
            for c in range(cores)
            for z in range(chips)
        ]
        return lax.ppermute(value, AXES, pairs)

    def core(self, value):
        return self.permute(value, lambda g, p, c, z: (g, p, 1 - c, z))

    def chip(self, value, bit):
        return self.permute(value, lambda g, p, c, z: (g, p, c, z ^ bit))

    def column(self, value, bit):
        return self.permute(value, lambda g, p, c, z: (g, p ^ bit, c, z))

    def in_order(self, mine, other):
        return jnp.where(self.c == 0, jnp.concatenate([mine, other]), jnp.concatenate([other, mine]))

    @staticmethod
    def shuffle(blocks, index):
        odd = (index % 2) == 1
        high = index >= 2
        blocks = [jnp.where(odd, blocks[j ^ 1], blocks[j]) for j in range(4)]
        return [jnp.where(high, blocks[j ^ 2], blocks[j]) for j in range(4)]

    def to_rows(self, block, mark=None, tie=None):
        quarter = block.shape[0] // 4
        got, sends = [], []
        for k in range(4):
            spot = self.z ^ k
            which = jnp.where(spot == 0, 0, jnp.where(spot == 1, 3, spot - 1))
            if mark is not None:
                which = which + jnp.isnan(mark[0, 0]).astype(jnp.int32)
            sends.append(lax.dynamic_slice_in_dim(block, which * quarter, quarter, 0).astype(bf16))
        tied = None if tie is None else hold(tie, *sends)
        for k in range(4):

            def target(g, p, c, z, k=k):
                t = z ^ k
                return (g, p, t % 2, 2 * c + t // 2)

            got.append(self.permute(sends[k], target))
        return got if tie is None else (got, tied)

    def column_blocks(self, rows):
        width = rows[0].shape[1] // 4
        sends = []
        for value in rows:
            blocks = [value[:, j * width : (j + 1) * width].astype(bf16) for j in range(4)]
            sends.append(self.shuffle(blocks, self.spot))
        return [jnp.stack([send[k] for send in sends]) for k in range(4)]

    def to_columns(self, sends):
        got = []
        for k in range(4):

            def target(g, p, c, z, k=k):
                t = 2 * (z % 2) + c
                return (g, p, z // 2, t ^ k)

            got.append(self.permute(sends[k], target))
        return got

    def whole_columns(self, got):
        parts = self.shuffle(got, self.z)
        whole = jnp.concatenate([parts[0], parts[2], parts[3], parts[1]], axis=1).astype(f32)
        return [whole[i] for i in range(whole.shape[0])]


class Columns:
    def __init__(self, mv, rows):
        width = rows.shape[1] // 4
        self.mv = mv
        self.blocks = mv.shuffle([rows[:, j * width : (j + 1) * width].astype(bf16) for j in range(4)], mv.z)
        self.first = mv.chip(jnp.stack([self.blocks[1], self.blocks[3]]), 1)

    def two(self, *marks):
        second = hold(jnp.stack([self.blocks[2], self.first[1]]), *marks)
        self.second = self.mv.chip(second, 2)

    def finish(self, *marks):
        mv = self.mv
        own = jnp.stack([self.blocks[0], self.first[0]])
        home = mv.c == mv.z // 2
        stay, leave = jnp.where(home, own, self.second), jnp.where(home, self.second, own)
        third = mv.core(hold(leave, *marks))
        every = jnp.stack([stay, third]).reshape((4,) + own.shape[1:])
        spots = [2 * (core ^ mv.c) + (half ^ (mv.z % 2)) for half, core in ((0, 0), (1, 0), (1, 1), (0, 1))]
        whole = [lax.dynamic_index_in_dim(every, spot, 0, keepdims=False) for spot in spots]
        return jnp.concatenate(whole).astype(f32)


class Gather:
    def __init__(self, mv, piece):
        self.mv, self.piece = mv, piece
        self.one = mv.chip(piece, 1)
        self.three = mv.chip(piece, 3)

    def second(self, *marks):
        self.two = self.mv.chip(hold(self.three, *marks), 1)

    def chips(self):
        return jnp.stack([self.piece, self.one, self.two, self.three])

    def heads(self, rows):
        every = self.chips()[:, :rows].reshape((2, 2, rows) + self.piece.shape[1:])
        got = self.mv.core(lax.dynamic_index_in_dim(every, 1 - self.mv.c, 0, keepdims=False))
        own = lax.dynamic_index_in_dim(every, self.mv.c, 0, keepdims=False)
        return jnp.concatenate([own, got])


class Across:
    def __init__(self, mv, group, chip=0):
        self.mv, self.group, self.chip = mv, group, chip
        self.x = mv.column(group, 1)
        self.y = mv.column(group, 2)

    def corner(self, *marks):
        half = self.group.shape[0] // 2
        x, y = hold((self.x, self.y), *marks)
        self.low_send, self.high_send = x[:half], y[half:]
        return self.low_send, self.high_send

    def finish(self):
        half = self.group.shape[0] // 2
        low = self.mv.column(self.low_send, 2)
        high = self.mv.column(self.high_send, 1)
        chip = self.chip
        return [(self.group, 0, chip), (self.x, 1, chip), (self.y, 2, chip), (low, 3, chip), (high, 3, chip + half)]


def add(*terms):
    return sum(t.astype(f32) for t in terms).astype(bf16)


class Scatter:
    def __init__(self, mv, near, far, kept):
        self.mv, self.kept = mv, kept
        self.near_y = mv.column(near, 2)
        self.far_x = mv.column(far, 1)

    def two(self, *marks):
        self.near_y, self.far_x = hold((self.near_y, self.far_x), *marks)
        self.near_send = add(self.kept[1], self.near_y[1])
        self.far_send = add(self.kept[3], self.far_x[1])
        return self.near_send, self.far_send

    def three(self, *marks):
        near_x = self.mv.column(self.near_send, 1)
        far_y = self.mv.column(self.far_send, 2)
        self.near_x, self.far_y = hold((near_x, far_y), *marks)
        return self.near_x, self.far_y

    def chips(self):
        near = add(self.kept[0], self.near_y[0], self.near_x)
        far = add(self.kept[2], self.far_x[0], self.far_y)
        return [near[0], near[1], far[0], far[1]]


def sum_columns(mv, terms, *marks):
    got = [mv.column(terms[j], j) for j in (1, 2, 3)]
    return add(terms[0], *hold(got, *marks))


def sum_chips(mv, terms, *marks):
    got = [mv.chip(terms[s], s) for s in (1, 2, 3)]
    return add(terms[0], *hold(got, *marks))


def all_columns(mv, mine, *marks):
    four = [mine] + [mv.column(mine, j) for j in (1, 2, 3)]
    return four + [mv.core(hold(value, *marks)) for value in four]


def per_device(stream, seq_lens, w_qkv, b_qv, w_out, b_out, w_up, b_up, w_down, b_down, cotangent):
    groups = lax.axis_size("g")
    mv = Moves(groups, lax.axis_size("p"), lax.axis_size("mp"))
    p, c, z = mv.p, mv.c, mv.z
    length, local = stream.shape
    chips = lax.axis_size("mp")
    width = local * chips
    layers = w_qkv.shape[0]
    hidden = w_up.shape[2]
    size = width // HEADS
    quarter = length // 4
    tokens = 2 * quarter
    half_heads = 2 * local
    att = Attention(tokens, HEADS // 2, size)
    keep = (jnp.arange(width, dtype=jnp.int32) < width - 1).astype(f32)[None, :]
    step = hidden // (2 * PIECES)
    part = local // (2 * PIECES)
    every = range(layers)
    where = jnp.stack([p, c, z]).astype(jnp.int32)
    core = c.astype(jnp.int32)

    def spot_of(mark):
        spot = 2 * p + c
        return spot if mark is None else spot + jnp.isnan(mark[0, 0]).astype(jnp.int32)

    def head_piece(layer, mark=None):
        spot = spot_of(mark)
        cut = lax.dynamic_slice_in_dim(w_qkv[layer], spot * part, part, 2)
        cut = jnp.transpose(cut, (1, 2, 0)).reshape(3 * part, width)
        return jnp.concatenate([cut, lax.dynamic_slice_in_dim(w_out[layer], spot * part, part, 0)])

    def unit_piece(layer, mark=None):
        spot = spot_of(mark)
        up = lax.dynamic_slice_in_dim(w_up[layer], spot * step, step, 1).T
        return jnp.concatenate([up, lax.dynamic_slice_in_dim(w_down[layer], spot * step, step, 0)])

    flat = jnp.concatenate([b_qv.reshape(-1), b_out.reshape(-1), b_up.reshape(-1), b_down.reshape(-1)])
    flat = flat.reshape(-1, width)
    high = flat.astype(bf16)
    low = (flat - high.astype(f32)).astype(bf16)
    heads = Gather(mv, jnp.concatenate([head_piece(0), high, low]))

    blocks = mv.to_rows(stream)
    heads.second()
    gathered = heads.chips()
    biases = gathered[:, 4 * part :].astype(f32).reshape(chips, 2, -1)
    biases = biases[:, 0] + biases[:, 1]
    heads = Across(mv, heads.heads(4 * part))
    x_mine, n_mine = quarter_rows(hold(blocks, heads.group), mv.spot, True)
    n_far = mv.chip(n_mine, 1)
    x, n = both_rows(hold(x_mine, *heads.corner()), mv.core(x_mine), core)
    biases = jnp.concatenate([lax.dynamic_index_in_dim(biases, z ^ i, 0) for i in range(4)])
    lens = jnp.where(c == z // 2, seq_lens, mv.core(seq_lens))
    flags = jnp.stack([(lens[0] > quarter).astype(jnp.int32), 1 - z % 2])
    units = Gather(mv, unit_piece(0, x))
    arrays = [place[0] for place in heads.finish()]
    arrays, n_far = hold((arrays, n_far), x)
    arrays = hold(arrays, n_far)
    head_rows = {0: heads_rows(arrays, where, 4, part, True)}

    cuts = [0, layers * 2 * local, layers * local, layers * hidden, layers * local]
    ends = [sum(cuts[: i + 1]) for i in range(5)]

    def bias(i, shape):
        return biases[:, ends[i] : ends[i + 1]].reshape((chips,) + shape)

    def bias_qv(layer):
        every_chip = bias(0, (layers, 2, local))[:, layer]
        pair = [2 * c, 2 * c + 1]
        if layer == 0:
            pair = [z ^ i for i in pair]
        two = jnp.stack([lax.dynamic_index_in_dim(every_chip, i, 0, keepdims=False) for i in pair], axis=1)
        return two.reshape(2, half_heads)

    def wide(i):
        return jnp.transpose(bias(i, (layers, local)), (1, 0, 2)).reshape(layers, width)

    bias_out, bias_down = wide(1), wide(3)
    all_up = lax.dynamic_index_in_dim(bias(2, (layers, PIECES, 2, step)), c, 3, keepdims=False)
    bias_up = jnp.transpose(all_up, (1, 0, 2, 3)).reshape(layers, chips * PIECES * step)

    saved = []
    outs = []
    pieces = {}
    scale = float(size) ** -0.5
    zero = jnp.zeros((half_heads,), f32)
    mult = jnp.concatenate([zero + scale, zero + 1.0, zero + 1.0])
    for layer in every:
        last = layer + 1 == layers
        rows, out_rows = head_rows[layer]
        pair = bias_qv(layer)
        offset = jnp.concatenate([pair[0], zero, pair[1]])
        proj = dot_nt(hold(n, units.three) if layer == 0 else n, rows)
        qkv = ((proj + offset).astype(bf16).astype(f32) * mult).astype(bf16)
        local_in = qkv
        if layer == 0:
            units.second(rows)
            group = hold(units.chips(), qkv)
            local_in, n_far = hold((qkv, n_far), group)
            local_in = hold(local_in, n_far)
            units = Across(mv, group)
        if last:
            cot_blocks, local_in = mv.to_rows(cotangent, n, local_in)
        acc, high, sums = att.forward_local(flags, local_in)
        if not last:
            piece = jnp.concatenate([unit_piece(layer + 1, n_mine), head_piece(layer + 1, n_mine)])
            piece = hold(piece, units.group) if layer == 0 else piece
            piece = hold(lax.all_gather(piece, "mp", axis=0), acc)
            more_heads = lax.all_gather(piece[:, 2 * step :], "p", axis=0)
            more_units = lax.all_gather(piece[:, : 2 * step], "p", axis=0)
        n_far = hold(n_far, acc)
        n_far_other = mv.core(n_far)
        kv = far_project(where, n_far, n_far_other, rows, offset[half_heads:])
        kv_in = kv
        if layer == 0:
            kv_in = hold(kv_in, units.corner(acc))
            finished = units.finish()
            pieces[0] = turned_units(finished)
        o, lse = att.forward_remote(flags, qkv, kv_in, acc, high, sums)
        out_in = hold(o, *finished) if layer == 0 else o
        out_in = hold(out_in, *cot_blocks) if last else out_in
        branch = dot_nn(out_in, out_rows).astype(bf16)
        branch_in = branch
        if layer == 1:
            sends = mv.column_blocks([outs[0]])
            branch_in = hold(branch, *sends)
            first_blocks = mv.to_columns(sends)
        x1, n1, g, slope, branch_two = mlp_forward(
            where, x, branch_in, mv.core(branch), bias_out[layer], pieces[layer], step, bias_up[layer]
        )
        if layer == 1:
            branch_two = hold(branch_two, *first_blocks)
        saved.append((x, n, n_far, n_far_other, qkv, kv, o, lse, x1, n1, g, slope))
        if not last:
            pieces[layer + 1] = plain_units(more_units)
            more_heads = hold(more_heads, branch_two)
            got = mv.core(lax.dynamic_slice_in_dim(more_heads, 2 * (1 - c), 2, 1))
            head_rows[layer + 1] = heads_rows([more_heads, got], where, 4, part, False)
        x, n = next_stream(x1, branch_two, mv.core(branch_two), bias_down[layer])
        if not last:
            n_far = mv.chip(lax.dynamic_slice_in_dim(n, c * quarter, quarter, 0), 1)
        if layer == 0 or last:
            outs.append(lax.dynamic_slice_in_dim(x, c * quarter, quarter, 0))

    def all_groups(value):
        return lax.psum(value, "g") if groups > 1 else value

    gb_q, gb_v, gb_out, gb_up, gb_down = {}, {}, {}, {}, {}
    unit_grads, head_grads = [], []

    def everywhere(mine, fast, *marks):
        mine = all_groups(mine)
        return all_columns(mv, mine, *marks) if fast else [lax.all_gather(mine, ("p", "c"), axis=0)]

    def end_units(layer, mine, fast, *marks):
        unit_grads[:] = units_out(where, layer, layers, everywhere(mine, fast, *marks), step, unit_grads)

    def end_heads(layer, mine, fast):
        got = heads_out(where, layer, layers, everywhere(mine, fast), part, head_grads)
        head_grads[:] = got[:2]
        return got[2]

    def summed(terms):
        return lax.psum_scatter(terms, "p", scatter_dimension=0)

    def summed_chips(mine):
        return lax.psum_scatter(mine, "mp", scatter_dimension=0)

    (cot_mine,) = quarter_rows(cot_blocks, mv.spot, False)
    def bias_rows():
        once = (c == 0).astype(f32)

        def by_chip(values):
            rows = jnp.stack([values[i][0] for i in every]).reshape(layers, chips, local) * once
            return jnp.transpose(rows, (1, 0, 2)).reshape(chips, -1)

        def own_chips(layer):
            two = jnp.stack([gb_q[layer], gb_v[layer]]).reshape(2, 2, local)
            rows = []
            for chip in range(chips):
                turned = (chip ^ z) if layer == 0 else chip
                value = lax.dynamic_index_in_dim(two, turned % 2, 1, keepdims=False)
                rows.append(jnp.where(turned // 2 == c, value, 0.0))
            return jnp.stack(rows)

        qv = jnp.stack([own_chips(i) for i in every], axis=1).reshape(chips, -1)
        up = jnp.stack([gb_up[i][0] for i in every]).reshape(layers, chips, PIECES, step)
        up = jnp.transpose(up, (1, 0, 2, 3))[:, :, :, None]
        none = jnp.zeros_like(up)
        up = jnp.where(c == 0, jnp.concatenate([up, none], axis=3), jnp.concatenate([none, up], axis=3))
        flat = jnp.concatenate([qv, by_chip(gb_out), up.reshape(chips, -1), by_chip(gb_down)], axis=1)
        return flat

    sends = mv.column_blocks([outs[-1]])
    before = (hold(cot_mine, *sends), mv.core(cot_mine))
    out_blocks = mv.to_columns(sends)
    later_sums = None
    for layer in reversed(every):
        x, n, n_far, n_far_other, qkv, kv, o, lse, x1, n1, g, slope = saved[layer]
        rows, out_rows = head_rows[layer]
        if layer == 0 and later_sums is not None:
            before = (hold(before[0], later_sums[1]),) + before[1:]
        got = mlp_backward(where, before, n1, g, slope, pieces[layer], step)
        dx, dn1, terms, (gb_up[layer], gb_down[layer]) = got[0], got[1], got[2:-2], got[-2:]
        if layer == 0:
            unit_sums = Scatter(mv, *terms)
        else:
            columns_sum = summed(terms[0])
        dx1, da, do, gb_out[layer] = out_backward(dx, x1, dn1, mv.core(dn1), out_rows)
        if layer == 0 and later_sums is not None:
            done = summed_chips(hold(later_sums[1], later_sums[3]))
        dqt, dkr, dvr, inner, far_sums = att.backward_remote(flags, qkv, kv, o, do, lse)
        far_send, far_keep = far_terms(where, dkr, dvr, rows)
        far_sum = add(far_keep, mv.core(far_send))
        back = mv.chip(far_sum, 1)
        local_dqt = hold(dqt, far_sum)
        if layer == 0 and later_sums is not None:
            local_dqt = hold(local_dqt, done)
        if layer == 0:
            local_dqt = hold(local_dqt, unit_sums.two(far_send))
        dq, dk, dv, near_sums = att.backward_local(flags, qkv, do, lse, inner, local_dqt)
        if layer == 0 and later_sums is not None:
            done_heads = summed_chips(hold(later_sums[2], dq))
            end_units(later_sums[0], done, False)
        gb_q[layer] = near_sums[:, 0].reshape(-1)
        gb_v[layer] = (near_sums[:, 1] + far_sums[:, 0]).reshape(-1)
        terms_in = hold(dq, *out_blocks) if layer == layers - 1 else dq
        if layer == 0:
            terms_in = hold(terms_in, back, unit_sums.three(dq))
            if later_sums is not None:
                terms_in = hold(terms_in, later_sums[2])
        terms = heads_terms(where, terms_in, dk, dv, o, dkr, dvr, n, n_far, n_far_other, da, part, layer == 0)
        if layer > 0:
            dn = near_terms(where, hold(dq, terms), dk, dv, back, rows)
            mine, got = terms[0], mv.core(hold(terms[1], dn))
            whole = jnp.where(
                c == 0, jnp.concatenate([mine, got], axis=1), jnp.concatenate([got, mine], axis=1)
            )
            later_sums = (layer, columns_sum, summed(hold(whole, columns_sum)), dq)
        else:
            head_terms = terms
            unit_mine = unit_sums.chips()
            beside = mv.chip(jnp.stack([unit_mine[1], unit_mine[2]]), 1)
            beside = hold(beside, terms)
            across = add(unit_mine[3], beside[1])
            dn = near_terms(where, hold(dq, across), dk, dv, back, rows)
            unit_last = mv.chip(across, 3)
        before = (dx1, x, dn, mv.core(dn))
    dx1, x, dn, dn_other = before
    mine = lambda value: lax.dynamic_slice_in_dim(value, c * quarter, quarter, 0)
    dx = mine(dx1) + norm_back(mine(x), mine(dn).astype(f32) + mine(dn_other).astype(f32))
    head_got = [mv.column(head_terms[j], j) for j in (1, 2, 3)]
    columns = Columns(mv, dx * keep)
    head_got = hold(head_got, columns.first, unit_last, *unit_grads)
    unit_sum = add(unit_mine[0], beside[0], hold(unit_last, head_got))
    head_sum = add(head_terms[0], *head_got)
    head_pair = head_sum[2:]
    got = mv.core(head_pair)
    pair, other = jnp.where(c == 0, head_sum[:2], got), jnp.where(c == 0, got, head_sum[:2])
    flat = bias_rows()
    extra = jnp.concatenate([flat, jnp.zeros_like(flat)], axis=1).reshape(chips, -1, width)
    extra = [lax.dynamic_index_in_dim(extra, z ^ i, 0, keepdims=False).astype(bf16) for i in range(chips)]
    terms = [jnp.concatenate(two) for two in zip((pair[0], pair[1], other[0], other[1]), extra)]
    beside = mv.chip(jnp.stack([terms[1], terms[2]]), 1)
    across = add(terms[3], beside[1])
    head_sum = add(terms[0], beside[0], mv.chip(across, 3))
    columns.two(across)
    grad_stream = columns.finish(head_sum)
    end_units(0, hold(unit_sum, across), True, head_sum)
    bias_sums = end_heads(0, head_sum, True)
    if later_sums is not None:
        end_heads(later_sums[0], hold(done_heads, head_sum), False)
    outs = [mv.whole_columns(got)[0] for got in (first_blocks, out_blocks)]

    flat = bias_sums[: ends[4] // width].reshape(-1)
    pieces = [flat[ends[i] : ends[i + 1]] for i in range(4)]
    return (
        outs[0],
        outs[1],
        grad_stream,
        jnp.transpose(head_grads[0], (0, 3, 1, 2)),
        pieces[0].reshape(layers, 2, local),
        head_grads[1],
        pieces[1].reshape(layers, local),
        unit_grads[0],
        pieces[2].reshape(layers, hidden),
        unit_grads[1],
        pieces[3].reshape(layers, local),
    )


def solution(mesh):
    rows, chips = mesh.shape["dp"], mesh.shape["mp"]
    grid = Mesh(mesh.devices.reshape(rows // (2 * PIECES), PIECES, 2, chips), AXES)
    dp = ("g", "p", "c")
    in_specs = (
        P(dp, "mp"),
        P(dp),
        P(None, None, None, "mp"),
        P(None, None, "mp"),
        P(None, "mp", None),
        P(None, "mp"),
        P(None, None, "mp"),
        P(None, "mp"),
        P(None, "mp", None),
        P(None, "mp"),
        P(dp, "mp"),
    )
    out_specs = (
        P(dp, "mp"),
        P(dp, "mp"),
        P(dp, "mp"),
        P(None, None, None, "mp"),
        P(None, None, "mp"),
        P(None, "mp", None),
        P(None, "mp"),
        P(None, None, "mp"),
        P(None, "mp"),
        P(None, "mp", None),
        P(None, "mp"),
    )
    return jax.shard_map(per_device, mesh=grid, in_specs=in_specs, out_specs=out_specs, check_vma=False)
```

time: 951 us -> 646 us (0.68)
  waiting for transfers between devices: 321 us -> 132 us
  Pallas kernels: 92.8 us -> 260 us
  blocking collectives: 142 us -> 0 us
  matrix products: 133 us -> 15.6 us
  other arithmetic: 118 us -> 33.9 us
  starting transfers between devices: 64.8 us -> 107 us
    pallas_call x0 -> x25, Pallas kernels: none -> 194 us  [the longest x22 184 us: staged(): kernel_call(kernel, us, size // 2 ** 20 + 12, smem() * len(scalars) + hbm...]
    reduce_scatter x12 -> x2, waiting for transfers between devices: 174 us -> 0.01 us  [summed_chips(): return lax.psum_scatter(mine, 'mp', scatter_dimension=0)]
    all_gather x6 -> x0, blocking collectives: 142 us -> none  [the longest x4 104 us: gather_units(): lax.all_gather(rows, 'mp', axis=0, tiled=True)]
    reduce_sum x17 -> x1, other arithmetic: 64.9 us -> 1.87 us  [norm_of(): squares = jnp.sum(x * x, axis=1, keepdims=True)]
    ppermute x51 -> x81, starting transfers between devices: 62.6 us -> 105 us  [permute(): return lax.ppermute(value, AXES, pairs)]
    dot_general x10 -> x2, matrix products: 51.4 us -> 10.2 us  [dot_nt(): return lax.dot_general(a, b, COLS_T, preferred_element_type=f32)]
    all_gather x11 -> x5, waiting for transfers between devices: 54.8 us -> 13.6 us  [the longest x1 7.85 us: per_device(): more_heads = lax.all_gather(piece[:, 2 * step:], 'p', axis=0)]
    dot_general x12 -> x0, matrix products: 40.1 us -> none  [dot_tn(): return lax.dot_general(a, b, ROWS_T, preferred_element_type=f32)]
  transfers between devices with their start and end apart: 74 -> 90, of which waited for: 27 -> 32; matrix products, arithmetic and copies ran while one was open for 26% -> 16% of each run, Pallas kernels for 9% -> 37%
where the time goes in v2:
time: 646 us; the launch traced here: 637 us
  Pallas kernels  260 us (40%)
  waiting for transfers between devices  132 us (20%)
  starting transfers between devices  107 us (17%)
  local copies, waits for them, and re-layouts  68.1 us (11%)
  other arithmetic  33.9 us (5%)
  between operations  20.1 us (3%)
  matrix products  15.6 us (2%)
    pallas_call x22, Pallas kernels, staged(): kernel_call(kernel, us, size // 2 ** 20 + 12, smem() * len(scalars) + hbm...  184 us
    ppermute x81, waiting for transfers between devices, permute(): return lax.ppermute(value, AXES, pairs)  117 us
    ppermute x81, starting transfers between devices, permute(): return lax.ppermute(value, AXES, pairs)  105 us
    pallas_call x2, Pallas kernels, backward_local(): self.call(functools.partial(bwd_local_kernel, self.quarter, self.size, fl...  23.8 us
    unnamed x170, local copies, waits for them, and re-layouts  20.6 us
    pallas_call x2, Pallas kernels, forward_local(): self.call(functools.partial(fwd_local_kernel, self.quarter, self.size), [...  18.1 us
  transfers between devices with their start and end apart: 90, of which 32 were waited for; matrix products, arithmetic and copies ran while one was open for 16% of the time, Pallas kernels for 37%

profile of v2, /device:TPU:0, one launch (start us, length us, event | category | flops | bytes accessed | tf_op | source)
XLA Modules:
  0.0 636.5 jit_solution(11462070104296543414)
XLA Ops:
  60.5 7.1 %collective-permute-done.8.refs_2_ = bf16[4,96,768]{2,1,0:T(8,128)(2,1)} collective-permute-done((bf16[4,96,768]{2,1,0:T(8,128)(2,1)S(1)}, bf16[4,96,768]{2,1,0:T(8,128)(2,1)}, u32[]{:S(2)}, u32[]{:S(2)}) %collective-permute-start.8) | collective-permute-done | bytes 589856 | tf_op jit(solution)/shard_map/ppermute | solution.py:1042
  88.6 5.8 collective-permute-done.12
  106.7 9.0 %shard_map.197 = (f32[1024,384]{1,0:T(8,128)}, f32[1024,384]{1,0:T(8,128)}, f32[1024,384]{1,0:T(8,128)}) custom-call(s32[2]{0:T(128)} %pad_add_fusion.1.s_ref, bf16[1024,1152]{1,0:T(8,128)(2,1)} %multiply_convert_fusion.1.q_ref.k_ref.v_ref, bf16[1024,1152]{1,0:T(8,128)(2,1)} %multiply_convert_fusion.1.q_ref.k_ref.v_ref, ...), custom_call_target="tpu_custom_call" | custom-call | flops 9200000000 | bytes 27600000 | tf_op jit(solution)/shard_map/pallas_call | solution.py:263
  119.1 5.6 shard_map.198.k_ref.v_ref
  124.7 9.1 %collective-permute-done.19.refs_7_.refs_9_ = bf16[4,192,768]{2,1,0:T(8,128)(2,1)S(1)} collective-permute-done((bf16[4,192,768]{2,1,0:T(8,128)(2,1)S(1)}, bf16[4,192,768]{2,1,0:T(8,128)(2,1)S(1)}, u32[]{:S(2)}, u32[]{:S(2)}) %collective-permute-start.19) | collective-permute-done | bytes 1179680 | tf_op jit(solution)/shard_map/ppermute | solution.py:1042
  136.2 5.8 all-gather.12.cloned.1.call-done
  144.0 6.0 shard_map.199
  155.9 15.1 %shard_map.200 = (f32[1024,768]{1,0:T(8,128)}, bf16[1024,768]{1,0:T(8,128)(2,1)}, bf16[1536,1024]{1,0:T(8,128)(2,1)}, bf16[1536,1024]{1,0:T(8,128)(2,1)}, bf16[1024,768]{1,0:T(8,128)(2,1)}) custom-call(s32[3]{0:T(128)} %pad_add_fusion.refs_0_, f32[1024,768]{1,0:T(8,128)} %get-tuple-element.171.refs_1_, bf16[1024,768]{1,0:T(8,128)(2,1)} %copy-done.48, ...), custom_call_target="tpu_custom_call" | custom-call | flops 14000000000 | bytes 42000000 | tf_op jit(solution)/shard_map/pallas_call | solution.py:480
  172.6 7.9 %all-gather.14.cloned.1.call-done = bf16[16,96,768]{2,1,0:T(8,128)(2,1)} async-done(((bf16[4,96,768]{2,1,0:T(8,128)(2,1)}), bf16[16,96,768]{2,1,0:T(8,128)(2,1)}) %all-gather.14.cloned.1.call-update) | async-done | bytes 2359312 | tf_op jit(solution)/shard_map/all_gather | solution.py:1320
  204.6 9.1 %shard_map.203 = (f32[1024,384]{1,0:T(8,128)}, f32[1024,384]{1,0:T(8,128)}, f32[1024,384]{1,0:T(8,128)}) custom-call(s32[2]{0:T(128)} %pad_add_fusion.1.s_ref, bf16[1024,1152]{1,0:T(8,128)(2,1)} %multiply_convert_fusion.q_ref.k_ref.v_ref, bf16[1024,1152]{1,0:T(8,128)(2,1)} %multiply_convert_fusion.q_ref.k_ref.v_ref, ...), custom_call_target="tpu_custom_call" | custom-call | flops 9200000000 | bytes 27600000 | tf_op jit(solution)/shard_map/pallas_call | solution.py:263
  215.7 7.6 %collective-permute-start.33 = (bf16[512,192]{1,0:T(8,128)(2,1)S(1)}, bf16[512,192]{1,0:T(8,128)(2,1)S(1)}, u32[]{:S(2)}, u32[]{:S(2)}) collective-permute-start(bf16[512,192]{1,0:T(8,128)(2,1)S(1)} %copy-done.24), channel_id=1, source_target_pairs={{0,4},{1,0},{2,5},{3,1},{4,6},{5,2},{6,7},{7,3},{8,12},{9,8},{10,1... | collective-permute-start | bytes 589832 | tf_op jit(solution)/shard_map/ppermute | solution.py:1042
  232.0 5.6 shard_map.205
  237.7 6.6 %collective-permute-done.34.refs_2_ = bf16[512,192]{1,0:T(8,128)(2,1)S(1)} collective-permute-done((bf16[512,192]{1,0:T(8,128)(2,1)S(1)}, bf16[512,192]{1,0:T(8,128)(2,1)S(1)}, u32[]{:S(2)}, u32[]{:S(2)}) %collective-permute-start.34) | collective-permute-done | bytes 196640 | tf_op jit(solution)/shard_map/ppermute | solution.py:1042
  260.7 15.0 %shard_map.206 = (f32[1024,768]{1,0:T(8,128)}, bf16[1024,768]{1,0:T(8,128)(2,1)}, bf16[1536,1024]{1,0:T(8,128)(2,1)}, bf16[1536,1024]{1,0:T(8,128)(2,1)}, bf16[1024,768]{1,0:T(8,128)(2,1)}) custom-call(s32[3]{0:T(128)} %pad_add_fusion.refs_0_, f32[1024,768]{1,0:T(8,128)} %get-tuple-element.204.refs_1_.refs_2_, ...), custom_call_target="tpu_custom_call" | custom-call | flops 14000000000 | bytes 42000000 | tf_op jit(solution)/shard_map/pallas_call | solution.py:480
  275.8 5.6 collective-permute-start.37
  292.9 19.5 %shard_map.209 = (f32[1024,768]{1,0:T(8,128)}, bf16[1024,768]{1,0:T(8,128)(2,1)}, bf16[4,4,192,768]{3,2,1,0:T(8,128)(2,1)}, f32[8,1536]{1,0:T(8,128)}, f32[8,768]{1,0:T(8,128)}) custom-call(s32[3]{0:T(128)} %pad_add_fusion.refs_0_, bf16[512,768]{1,0:T(8,128)(2,1)} %shard_map.208.refs_1_, bf16[512,768]{1,0:T(8,128)(2,1)} %collective-permute-done.42.refs_2_, ...), custom_call_target="tpu_custom_call" | custom-call | flops 17999998976 | bytes 54000000 | tf_op jit(solution)/shard_map/pallas_call | solution.py:480
  317.6 8.8 %shard_map.210 = (f32[1024,768]{1,0:T(8,128)}, bf16[1024,768]{1,0:T(8,128)(2,1)}, bf16[1024,384]{1,0:T(8,128)(2,1)}, f32[8,768]{1,0:T(8,128)}) custom-call(f32[1024,768]{1,0:T(8,128)} %get-tuple-element.227.refs_0_, f32[1024,768]{1,0:T(8,128)} %get-tuple-element.219.refs_0_.refs_1_, bf16[1024,768]{1,0:T(8,128)(2,1)} %get-tuple-element.228.refs_2_, ...), custom_call_target="tpu_custom_call" | custom-call | flops 5000000000 | bytes 15000000 | tf_op jit(solution)/shard_map/pallas_call | solution.py:480
  326.5 6.0 shard_map.211
  338.3 9.8 %collective-permute-start.38 = (bf16[1,512,192]{2,1,0:T(8,128)(2,1)S(1)}, bf16[1,512,192]{2,1,0:T(8,128)(2,1)}, u32[]{:S(2)}, u32[]{:S(2)}) collective-permute-start(bf16[1,512,192]{2,1,0:T(8,128)(2,1)S(1)} %get-tuple-element.418), channel_id=1, source_target_pairs={{0,3},{1,1},{2,7},{3,5},{4,2},{5,0},{6,6},{7,4},{8,11},{9,9},{10,1... | collective-permute-start | bytes 589832 | tf_op jit(solution)/shard_map/ppermute | solution.py:1042
  355.2 11.8 %shard_map.213 = (bf16[1024,384]{1,0:T(8,128)(2,1)}, bf16[1024,384]{1,0:T(8,128)(2,1)}, bf16[1024,384]{1,0:T(8,128)(2,1)}, f32[3,8,128]{2,1,0:T(8,128)}) custom-call(s32[2]{0:T(128)} %pad_add_fusion.1.s_ref, bf16[1024,1152]{1,0:T(8,128)(2,1)} %multiply_convert_fusion.q_ref.k_ref.v_ref, bf16[1024,1152]{1,0:T(8,128)(2,1)} %multiply_convert_fusion.q_ref.k_ref.v_ref, ...), custom_call_target="tpu_custom_call" | custom-call | flops 20000000000 | bytes 60000000 | tf_op jit(solution)/shard_map/pallas_call | solution.py:305
  368.7 11.9 %shard_map.214 = (bf16[4,2,96,768]{3,2,1,0:T(8,128)(2,1)}, bf16[4,2,96,768]{3,2,1,0:T(8,128)(2,1)}) custom-call(s32[3]{0:T(128)} %pad_add_fusion.refs_0_, bf16[1024,384]{1,0:T(8,128)(2,1)} %get-tuple-element.248.refs_1_, bf16[1024,384]{1,0:T(8,128)(2,1)} %get-tuple-element.243.refs_2_, bf16[1024,384]{1,0:T(8,128)(2,1)} %get-tuple-element.244.refs_3_, ...), custom_call_target="tpu_custom_call" | custom-call | flops 6000000000 | bytes 18000000 | tf_op jit(solution)/shard_map/pallas_call | solution.py:480
  386.1 6.8 %shard_map.215.refs_3_ = bf16[1024,768]{1,0:T(8,128)(2,1)} custom-call(s32[3]{0:T(128)} %pad_add_fusion.refs_0_, bf16[1024,384]{1,0:T(8,128)(2,1)} %get-tuple-element.248.refs_1_, bf16[1024,384]{1,0:T(8,128)(2,1)} %get-tuple-element.243.refs_2_, bf16[1024,384]{1,0:T(8,128)(2,1)} %get-tuple-element.244.refs_3_, ...), custom_call_target="tpu_custom_call" | custom-call | flops 3000000000 | bytes 9000000 | tf_op jit(solution)/shard_map/pallas_call | solution.py:480
  400.4 21.9 %shard_map.216 = (f32[1024,768]{1,0:T(8,128)}, bf16[1024,768]{1,0:T(8,128)(2,1)}, bf16[2,2,192,768]{3,2,1,0:T(8,128)(2,1)}, bf16[2,2,192,768]{3,2,1,0:T(8,128)(2...) custom-call(s32[3]{0:T(128)} %pad_add_fusion.refs_0_, ...), custom_call_target="tpu_custom_call" | custom-call | flops 17999998976 | bytes 54000000 | tf_op jit(solution)/shard_map/pallas_call | solution.py:480
  433.7 8.7 %shard_map.217 = (f32[1024,768]{1,0:T(8,128)}, bf16[1024,768]{1,0:T(8,128)(2,1)}, bf16[1024,384]{1,0:T(8,128)(2,1)}, f32[8,768]{1,0:T(8,128)}) custom-call(f32[1024,768]{1,0:T(8,128)} %get-tuple-element.252.refs_0_, f32[1024,768]{1,0:T(8,128)} %get-tuple-element.202.refs_0_.refs_1_, bf16[1024,768]{1,0:T(8,128)(2,1)} %get-tuple-element.253.refs_2_, ...), custom_call_target="tpu_custom_call" | custom-call | flops 5000000000 | bytes 15000000 | tf_op jit(solution)/shard_map/pallas_call | solution.py:480
  442.4 5.9 shard_map.218
  457.3 7.5 %collective-permute-done.49 = bf16[2,2,192,768]{3,2,1,0:T(8,128)(2,1)S(1)} collective-permute-done((bf16[2,2,192,768]{3,2,1,0:T(8,128)(2,1)}, bf16[2,2,192,768]{3,2,1,0:T(8,128)(2,1)S(1)}, u32[]{:S(2)}, u32[]{:S(2)}) %collective-permute-start.49) | collective-permute-done | bytes 1179680 | tf_op jit(solution)/shard_map/ppermute | solution.py:1042
  476.5 12.0 %shard_map.220 = (bf16[1024,384]{1,0:T(8,128)(2,1)}, bf16[1024,384]{1,0:T(8,128)(2,1)}, bf16[1024,384]{1,0:T(8,128)(2,1)}, f32[3,8,128]{2,1,0:T(8,128)}) custom-call(s32[2]{0:T(128)} %pad_add_fusion.1.s_ref, bf16[1024,1152]{1,0:T(8,128)(2,1)} %multiply_convert_fusion.1.q_ref.k_ref.v_ref, bf16[1024,1152]{1,0:T(8,128)(2,1)} %multiply_convert_fusion.1.q_ref.k_ref.v_ref, ...), custom_call_target="tpu_custom_call" | custom-call | flops 20000000000 | bytes 60000000 | tf_op jit(solution)/shard_map/pallas_call | solution.py:305
  496.3 11.9 %shard_map.221 = (bf16[4,96,768]{2,1,0:T(8,128)(2,1)}, bf16[4,96,768]{2,1,0:T(8,128)(2,1)}, bf16[4,96,768]{2,1,0:T(8,128)(2,1)}, bf16[4,96,768]{2,1,0:T(8,128)(2,1)}) custom-call(s32[3]{0:T(128)} %pad_add_fusion.refs_0_, bf16[1024,384]{1,0:T(8,128)(2,1)} %get-tuple-element.285.refs_1_, bf16[1024,384]{1,0:T(8,128)(2,1)} %get-tuple-element.277.refs_2_, ...), custom_call_target="tpu_custom_call" | custom-call | flops 6000000000 | bytes 18000000 | tf_op jit(solution)/shard_map/pallas_call | solution.py:480
  509.1 7.0 %shard_map.222 = bf16[1024,768]{1,0:T(8,128)(2,1)} custom-call(s32[3]{0:T(128)} %pad_add_fusion.refs_0_, bf16[1024,384]{1,0:T(8,128)(2,1)} %get-tuple-element.285.refs_1_, bf16[1024,384]{1,0:T(8,128)(2,1)} %get-tuple-element.277.refs_2_, bf16[1024,384]{1,0:T(8,128)(2,1)} %get-tuple-element.278.refs_3_, bf16[512,768]{1,0:T(8,128)(2,1)} %collective-permute-done.54.refs_4_, ...), custom_call_target="tpu_custom_call" | custom-call | flops 3000000000 | bytes 9000000 | tf_op jit(solution)/shard_map/pallas_call | solution.py:480
  540.7 12.7 %collective-permute-done.59 = bf16[4,96,768]{2,1,0:T(8,128)(2,1)} collective-permute-done((bf16[4,96,768]{2,1,0:T(8,128)(2,1)}, bf16[4,96,768]{2,1,0:T(8,128)(2,1)}, u32[]{:S(2)}, u32[]{:S(2)}) %collective-permute-start.59) | collective-permute-done | bytes 589856 | tf_op jit(solution)/shard_map/ppermute | solution.py:1042
  561.1 14.6 %collective-permute-done.63 = bf16[2,104,768]{2,1,0:T(8,128)(2,1)S(1)} collective-permute-done((bf16[2,104,768]{2,1,0:T(8,128)(2,1)S(1)}, bf16[2,104,768]{2,1,0:T(8,128)(2,1)S(1)}, u32[]{:S(2)}, u32[]{:S(2)}) %collective-permute-start.63) | collective-permute-done | bytes 319520 | tf_op jit(solution)/shard_map/ppermute | solution.py:1042
  597.3 8.6 %collective-permute-done.64 = bf16[2,512,192]{2,1,0:T(8,128)(2,1)} collective-permute-done((bf16[2,512,192]{2,1,0:T(8,128)(2,1)}, bf16[2,512,192]{2,1,0:T(8,128)(2,1)}, u32[]{:S(2)}, u32[]{:S(2)}) %collective-permute-start.64) | collective-permute-done | bytes 393248 | tf_op jit(solution)/shard_map/ppermute | solution.py:1042
  (531 shorter events, 310.2 us)
Async XLA Ops:
  7.2 134.8 %all-gather.12.cloned.1.call-start = ((), (), s32[]{:S(2)}) async-start(), calls=%async_computation.7 | async-start | bytes 2211840 | tf_op jit(solution)/shard_map/all_gather | solution.py:1319
  19.7 23.5 %collective-permute-start = (bf16[512,192]{1,0:T(8,128)(2,1)}, bf16[512,192]{1,0:T(8,128)(2,1)}, u32[]{:S(2)}, u32[]{:S(2)}) collective-permute-start(bf16[512,192]{1,0:T(8,128)(2,1)} %copy.105), channel_id=1, source_target_pairs={{0,0},{1,4},{2,1},{3,5},{4,2},{5,6},{6,3},{7,7},{8,8},{9,12},{10,9... | collective-permute-start | bytes 589832 | tf_op jit(solution)/shard_map/ppermute | solution.py:1042
  24.1 19.1 %collective-permute-start.1 = (bf16[512,192]{1,0:T(8,128)(2,1)}, bf16[512,192]{1,0:T(8,128)(2,1)}, u32[]{:S(2)}, u32[]{:S(2)}) collective-permute-start(bf16[512,192]{1,0:T(8,128)(2,1)} %copy.106), channel_id=1, source_target_pairs={{0,4},{1,0},{2,5},{3,1},{4,6},{5,2},{6,7},{7,3},{8,12},{9,8},{10,1... | collective-permute-start | bytes 589832 | tf_op jit(solution)/shard_map/ppermute | solution.py:1042
  50.1 23.3 %collective-permute-start.10 = (bf16[512,768]{1,0:T(8,128)(2,1)}, bf16[512,768]{1,0:T(8,128)(2,1)}, u32[]{:S(2)}, u32[]{:S(2)}) collective-permute-start(bf16[512,768]{1,0:T(8,128)(2,1)} %get-tuple-element.170.mine_ref), channel_id=1, source_target_pairs={{0,4},{1,5},{2,6},{3,7},{4,0},{5,1},{6,2},{7,3},{8,12},{9,13},{10,... | collective-permute-start | bytes 2359304 | tf_op jit(solution)/shard_map/ppermute | solution.py:1042
  56.3 28.0 %collective-permute-start.15 = (bf16[512,768]{1,0:T(8,128)(2,1)}, bf16[512,768]{1,0:T(8,128)(2,1)}, u32[]{:S(2)}, u32[]{:S(2)}) collective-permute-start(bf16[512,768]{1,0:T(8,128)(2,1)} %get-tuple-element.174), channel_id=1, source_target_pairs={{0,1},{1,0},{2,3},{3,2},{4,5},{5,4},{6,7},{7,6},{8,9},{9,8},{10,11... | collective-permute-start | bytes 2359304 | tf_op jit(solution)/shard_map/ppermute | solution.py:1042
  103.6 76.9 %all-gather.14.cloned.1.call-start = ((), (), s32[]{:S(2)}) async-start(), calls=%async_computation.8 | async-start | bytes 2949120 | tf_op jit(solution)/shard_map/all_gather | solution.py:1320
  105.7 28.1 %collective-permute-start.19 = (bf16[4,192,768]{2,1,0:T(8,128)(2,1)S(1)}, bf16[4,192,768]{2,1,0:T(8,128)(2,1)S(1)}, u32[]{:S(2)}, u32[]{:S(2)}) collective-permute-start(bf16[4,192,768]{2,1,0:T(8,128)(2,1)S(1)} %pad_maximum_fusion.refs_6_.refs_8_), channel_id=1, source_target_pairs={{0,8},{1,9},{2,10},{3,11},{4,12},{5,13},{6,14},{7,15},{8,0},{9,1},... | collective-permute-start | bytes 3538952 | tf_op jit(solution)/shard_map/ppermute | solution.py:1042
  106.3 27.8 %collective-permute-start.20 = (bf16[4,192,768]{2,1,0:T(8,128)(2,1)S(1)}, bf16[4,192,768]{2,1,0:T(8,128)(2,1)S(1)}, u32[]{:S(2)}, u32[]{:S(2)}) collective-permute-start(bf16[4,192,768]{2,1,0:T(8,128)(2,1)S(1)} %pad_maximum_fusion.refs_6_.refs_8_), channel_id=1, source_target_pairs={{0,16},{1,17},{2,18},{3,19},{4,20},{5,21},{6,22},{7,23},{8,24},{9,... | collective-permute-start | bytes 3538952 | tf_op jit(solution)/shard_map/ppermute | solution.py:1042
  143.9 116.8 %all-gather.16.cloned.1.call-start = ((), (), s32[]{:S(2)}) async-start(), calls=%async_computation.9 | async-start | bytes 5898240 | tf_op jit(solution)/shard_map/all_gather | solution.py:1321
  172.4 196.2 %reduce-scatter.13.cloned.1.call-start = ((), (), s32[]{:S(2)}) async-start(), calls=%async_computation.11 | async-start | bytes 5898240
  194.3 20.0 %collective-permute-start.30 = (bf16[512,768]{1,0:T(8,128)(2,1)S(1)}, bf16[512,768]{1,0:T(8,128)(2,1)S(1)}, u32[]{:S(2)}, u32[]{:S(2)}) collective-permute-start(bf16[512,768]{1,0:T(8,128)(2,1)S(1)} %constant_dynamic-slice_fusion.12), channel_id=1, source_target_pairs={{0,1},{1,0},{2,3},{3,2},{4,5},{5,4},{6,7},{7,6},{8,9},{9,8},{10,11... | collective-permute-start | bytes 2359304 | tf_op jit(solution)/shard_map/ppermute | solution.py:1042
  215.0 22.7 %collective-permute-start.32 = (bf16[512,192]{1,0:T(8,128)(2,1)S(1)}, bf16[512,192]{1,0:T(8,128)(2,1)S(1)}, u32[]{:S(2)}, u32[]{:S(2)}) collective-permute-start(bf16[512,192]{1,0:T(8,128)(2,1)S(1)} %copy-done.25), channel_id=1, source_target_pairs={{0,0},{1,4},{2,1},{3,5},{4,2},{5,6},{6,3},{7,7},{8,8},{9,12},{10,9... | collective-permute-start | bytes 589832 | tf_op jit(solution)/shard_map/ppermute | solution.py:1042
  215.7 22.0 %collective-permute-start.33 = (bf16[512,192]{1,0:T(8,128)(2,1)S(1)}, bf16[512,192]{1,0:T(8,128)(2,1)S(1)}, u32[]{:S(2)}, u32[]{:S(2)}) collective-permute-start(bf16[512,192]{1,0:T(8,128)(2,1)S(1)} %copy-done.24), channel_id=1, source_target_pairs={{0,4},{1,0},{2,5},{3,1},{4,6},{5,2},{6,7},{7,3},{8,12},{9,8},{10,1... | collective-permute-start | bytes 589832 | tf_op jit(solution)/shard_map/ppermute | solution.py:1042
  223.3 21.0 %collective-permute-start.34 = (bf16[512,192]{1,0:T(8,128)(2,1)S(1)}, bf16[512,192]{1,0:T(8,128)(2,1)S(1)}, u32[]{:S(2)}, u32[]{:S(2)}) collective-permute-start(bf16[512,192]{1,0:T(8,128)(2,1)S(1)} %copy.113), channel_id=1, source_target_pairs={{0,1},{1,5},{2,0},{3,4},{4,3},{5,7},{6,2},{7,6},{8,9},{9,13},{10,8... | collective-permute-start | bytes 589832 | tf_op jit(solution)/shard_map/ppermute | solution.py:1042
  223.3 21.0 %collective-permute-start.35 = (bf16[512,192]{1,0:T(8,128)(2,1)S(1)}, bf16[512,192]{1,0:T(8,128)(2,1)S(1)}, u32[]{:S(2)}, u32[]{:S(2)}) collective-permute-start(bf16[512,192]{1,0:T(8,128)(2,1)S(1)} %copy.114), channel_id=1, source_target_pairs={{0,5},{1,1},{2,4},{3,0},{4,7},{5,3},{6,6},{7,2},{8,13},{9,9},{10,1... | collective-permute-start | bytes 589832 | tf_op jit(solution)/shard_map/ppermute | solution.py:1042
  253.4 22.4 %collective-permute-start.25 = (bf16[1,512,192]{2,1,0:T(8,128)(2,1)S(1)}, bf16[1,512,192]{2,1,0:T(8,128)(2,1)S(1)}, u32[]{:S(2)}, u32[]{:S(2)}) collective-permute-start(bf16[1,512,192]{2,1,0:T(8,128)(2,1)S(1)} %get-tuple-element.422), channel_id=1, source_target_pairs={{0,3},{1,1},{2,7},{3,5},{4,2},{5,0},{6,6},{7,4},{8,11},{9,9},{10,1... | collective-permute-start | bytes 589832 | tf_op jit(solution)/shard_map/ppermute | solution.py:1042
  312.4 160.0 %reduce-scatter.9.cloned.1.call-start = ((), (), s32[]{:S(2)}) async-start(), calls=%async_computation.4 | async-start | bytes 1474560 | tf_op jit(solution)/shard_map/reduce_scatter | solution.py:1378
  338.3 28.7 %collective-permute-start.38 = (bf16[1,512,192]{2,1,0:T(8,128)(2,1)S(1)}, bf16[1,512,192]{2,1,0:T(8,128)(2,1)}, u32[]{:S(2)}, u32[]{:S(2)}) collective-permute-start(bf16[1,512,192]{2,1,0:T(8,128)(2,1)S(1)} %get-tuple-element.418), channel_id=1, source_target_pairs={{0,3},{1,1},{2,7},{3,5},{4,2},{5,0},{6,6},{7,4},{8,11},{9,9},{10,1... | collective-permute-start | bytes 589832 | tf_op jit(solution)/shard_map/ppermute | solution.py:1042
  353.3 32.8 %collective-permute-start.45 = (bf16[512,768]{1,0:T(8,128)(2,1)S(1)}, bf16[512,768]{1,0:T(8,128)(2,1)}, u32[]{:S(2)}, u32[]{:S(2)}) collective-permute-start(bf16[512,768]{1,0:T(8,128)(2,1)S(1)} %add_convert_fusion.3), channel_id=1, source_target_pairs={{0,1},{1,0},{2,3},{3,2},{4,5},{5,4},{6,7},{7,6},{8,9},{9,8},{10,11... | collective-permute-start | bytes 2359304 | tf_op jit(solution)/shard_map/ppermute | solution.py:1042
  368.6 127.7 %reduce-scatter.15.cloned.1.call-start = ((), (), s32[]{:S(2)}) async-start(), calls=%async_computation.12 | async-start | bytes 2949120
  399.9 132.8 %all-gather.10.cloned.1.call-start = ((), (), s32[]{:S(2)}) async-start(), calls=%async_computation.5 | async-start | bytes 2654208 | tf_op jit(solution)/shard_map/all_gather | solution.py:1364
  430.1 34.7 %collective-permute-start.49 = (bf16[2,2,192,768]{3,2,1,0:T(8,128)(2,1)}, bf16[2,2,192,768]{3,2,1,0:T(8,128)(2,1)S(1)}, u32[]{:S(2)}, u32[]{:S(2)}) collective-permute-start(bf16[2,2,192,768]{3,2,1,0:T(8,128)(2,1)} %get-tuple-element.265), channel_id=1, source_target_pairs={{0,16},{1,17},{2,18},{3,19},{4,20},{5,21},{6,22},{7,23},{8,24},{9,... | collective-permute-start | bytes 3538952 | tf_op jit(solution)/shard_map/ppermute | solution.py:1042
  430.1 36.7 %collective-permute-start.50 = (bf16[2,2,192,768]{3,2,1,0:T(8,128)(2,1)}, bf16[2,2,192,768]{3,2,1,0:T(8,128)(2,1)}, u32[]{:S(2)}, u32[]{:S(2)}) collective-permute-start(bf16[2,2,192,768]{3,2,1,0:T(8,128)(2,1)} %get-tuple-element.266), channel_id=1, source_target_pairs={{0,8},{1,9},{2,10},{3,11},{4,12},{5,13},{6,14},{7,15},{8,0},{9,1},... | collective-permute-start | bytes 3538952 | tf_op jit(solution)/shard_map/ppermute | solution.py:1042
  469.1 19.4 %collective-permute-start.51 = (bf16[2,192,768]{2,1,0:T(8,128)(2,1)}, bf16[2,192,768]{2,1,0:T(8,128)(2,1)S(1)}, u32[]{:S(2)}, u32[]{:S(2)}) collective-permute-start(bf16[2,192,768]{2,1,0:T(8,128)(2,1)} %get-tuple-element.383), channel_id=1, source_target_pairs={{0,8},{1,9},{2,10},{3,11},{4,12},{5,13},{6,14},{7,15},{8,0},{9,1},... | collective-permute-start | bytes 1769480 | tf_op jit(solution)/shard_map/ppermute | solution.py:1042
  472.4 113.1 %reduce-scatter.11.cloned.1.call-start = ((), (), s32[]{:S(2)}) async-start(), calls=%async_computation.6 | async-start | bytes 737280 | tf_op jit(solution)/shard_map/reduce_scatter | solution.py:1378
  475.0 21.3 %collective-permute-start.54 = (bf16[512,768]{1,0:T(8,128)(2,1)}, bf16[512,768]{1,0:T(8,128)(2,1)}, u32[]{:S(2)}, u32[]{:S(2)}) collective-permute-start(bf16[512,768]{1,0:T(8,128)(2,1)} %add_convert_fusion.2), channel_id=1, source_target_pairs={{0,1},{1,0},{2,3},{3,2},{4,5},{5,4},{6,7},{7,6},{8,9},{9,8},{10,11... | collective-permute-start | bytes 2359304 | tf_op jit(solution)/shard_map/ppermute | solution.py:1042
  525.3 28.1 %collective-permute-start.59 = (bf16[4,96,768]{2,1,0:T(8,128)(2,1)}, bf16[4,96,768]{2,1,0:T(8,128)(2,1)}, u32[]{:S(2)}, u32[]{:S(2)}) collective-permute-start(bf16[4,96,768]{2,1,0:T(8,128)(2,1)} %get-tuple-element.282), channel_id=1, source_target_pairs={{0,16},{1,17},{2,18},{3,19},{4,20},{5,21},{6,22},{7,23},{8,24},{9,... | collective-permute-start | bytes 1769480 | tf_op jit(solution)/shard_map/ppermute | solution.py:1042
  525.8 27.6 %collective-permute-start.60 = (bf16[4,96,768]{2,1,0:T(8,128)(2,1)}, bf16[4,96,768]{2,1,0:T(8,128)(2,1)}, u32[]{:S(2)}, u32[]{:S(2)}) collective-permute-start(bf16[4,96,768]{2,1,0:T(8,128)(2,1)} %get-tuple-element.283), channel_id=1, source_target_pairs={{0,24},{1,25},{2,26},{3,27},{4,28},{5,29},{6,30},{7,31},{8,16},{9,... | collective-permute-start | bytes 1769480 | tf_op jit(solution)/shard_map/ppermute | solution.py:1042
  532.2 21.3 %collective-permute-start.57 = (bf16[2,512,192]{2,1,0:T(8,128)(2,1)S(1)}, bf16[2,512,192]{2,1,0:T(8,128)(2,1)S(1)}, u32[]{:S(2)}, u32[]{:S(2)}) collective-permute-start(bf16[2,512,192]{2,1,0:T(8,128)(2,1)S(1)} %pad_maximum_fusion.5), channel_id=1, source_target_pairs={{0,1},{1,0},{2,3},{3,2},{4,5},{5,4},{6,7},{7,6},{8,9},{9,8},{10,11... | collective-permute-start | bytes 1179656 | tf_op jit(solution)/shard_map/ppermute | solution.py:1042
  555.3 70.1 %all-gather.18.cloned.1.call-start = ((), (), s32[]{:S(2)}) async-start(), calls=%async_computation.10 | async-start | bytes 1327104 | tf_op jit(solution)/shard_map/all_gather | solution.py:1364
  580.3 25.6 %collective-permute-start.64 = (bf16[2,512,192]{2,1,0:T(8,128)(2,1)}, bf16[2,512,192]{2,1,0:T(8,128)(2,1)}, u32[]{:S(2)}, u32[]{:S(2)}) collective-permute-start(bf16[2,512,192]{2,1,0:T(8,128)(2,1)} %pad_maximum_fusion.7), channel_id=1, source_target_pairs={{0,2},{1,3},{2,0},{3,1},{4,6},{5,7},{6,4},{7,5},{8,10},{9,11},{10,... | collective-permute-start | bytes 1179656 | tf_op jit(solution)/shard_map/ppermute | solution.py:1042
  594.2 22.5 %collective-permute-start.77 = (bf16[192,768]{1,0:T(8,128)(2,1)}, bf16[192,768]{1,0:T(8,128)(2,1)S(1)}, u32[]{:S(2)}, u32[]{:S(2)}) collective-permute-start(bf16[192,768]{1,0:T(8,128)(2,1)} %fusion.4.refs_1_), channel_id=1, source_target_pairs={{0,4},{1,5},{2,6},{3,7},{4,0},{5,1},{6,2},{7,3},{8,12},{9,13},{10,... | collective-permute-start | bytes 884744 | tf_op jit(solution)/shard_map/ppermute | solution.py:1042
  (135 other events, 1220.1 us)
Sparse Core Ops, SparseCore 0:
  103.7 38.2 all-gather.11
  144.1 36.3 all-gather.13
  182.3 57.0 all-gather.15
  312.5 56.0 reduce-scatter.12
  370.8 31.4 reduce-scatter.8
  405.2 45.0 reduce-scatter.14
  472.6 32.0 all-gather.9
  555.5 22.5 reduce-scatter.10
  585.7 32.3 all-gather.17
